TPU v7x, 256 devices: a whole 4x4x8 slice. The times are simulated.
256 devices in a mesh: row: 8 (over y, core), col: 32 (over z, x).
Axes of the slice: x: 4, y: 4, z: 8, core: 2. Of those that a mesh axis runs over, the one named last changes fastest.
Arguments:
- solution: float32 [8, 32, 16, 128, 128], P('row', 'col'), may hold values from -6 to 6
- residual: float32 [8, 32, 16, 128, 128], P('row', 'col'), may hold values from -6 to 6, as said below
- prev_direction: float32 [8, 32, 16, 128, 128], P('row', 'col'), may hold values from -6 to 6, as said below
- prev_dot: float32 [128], replicated, may hold values from 262144 to 1048576
- face_lists: int32 [8, 32, 4, 4], P('row', 'col'), may hold values from 0 to 16, as said below
- multiplicity: int32 [8, 32, 16], P('row', 'col'), may hold values from 1 to 2, as said below
- block_pattern: int32 [8, 32, 16, 3], P('row', 'col'), may hold values from 0 to 15, as said below
- schur: float32 [8, 32, 16, 3, 128, 128], P('row', 'col'), may hold values from -1 to 4, as said below
- neumann_inverse: float32 [8, 32, 16, 3, 128, 128], P('row', 'col'), may hold values from 0 to 2, as said below
- coarse_basis: float32 [8, 32, 8, 2048], P('row', 'col'), may hold values from -0.25 to 0.25
- primal_map: int32 [8, 32, 8], P('row', 'col'), may hold values from 0 to 1023, all different within a row
- coarse_inverse: float32 [1024, 1024], P('col'), may hold values from -1 to 1, as said below
Outputs:
- new_solution: float32 [8, 32, 16, 128, 128], P('row', 'col')
- new_residual: float32 [8, 32, 16, 128, 128], P('row', 'col')
- direction: float32 [8, 32, 16, 128, 128], P('row', 'col')
Inputs may be any that keep to these rules, and one draw needn't show every extreme that they name: face_lists[i, j, f, k] names the interface blocks that subdomain (i, j) shares with its neighbour across face f (0 toward row i-1, 1 toward row i+1, 2 toward column j-1, 3 toward column j+1); slot k of a face names the same unknowns as slot k of the neighbour's list for the facing face, and both lists have the same length, 1 to 4 blocks, none on faces at the grid's edge; unused slots hold 16; no block lies on two faces; some face holds 4 blocks. multiplicity is 2 for blocks named in face_lists and 1 for the others. block_pattern[i, j, b, 0] = b; the two other entries of block row b are two other blocks, each of which lists b in turn. `schur`: each subdomain's Schur complement is symmetric positive definite, with positive diagonal and no positive entry off it. `neumann_inverse`: each subdomain's local solve matrix is symmetric positive definite. `coarse_inverse`: symmetric positive definite. `residual`: copies of an unknown held by two subdomains (slot k of facing lists) are equal. `prev_direction`: copies of an unknown held by two subdomains (slot k of facing lists) are equal.
All inputs are finite; a program needn't handle non-finite values.
Results may differ from a plain program's by a relative error of at most 0.0003.
Values sent between devices are 32-bit elements; how exact they have to be, the bound alone decides.
A program may use at most 128 MiB of HBM per device.

v0:
```python
import jax
import jax.numpy as jnp
from jax import lax
from jax.sharding import PartitionSpec as P

HIGH = lax.Precision.HIGHEST


def extended(cells, sides, width):
    for axis, dim in sides:
        count = lax.axis_size(axis)
        ends = count - 1
        head = lax.slice_in_dim(cells, 0, width, axis=dim)
        tail = lax.slice_in_dim(cells, cells.shape[dim] - width, cells.shape[dim], axis=dim)
        cells = jnp.concatenate(
            [
                lax.ppermute(tail, axis, [(i, (i + 1) % count) for i in range(ends)]),
                cells,
                lax.ppermute(head, axis, [((i + 1) % count, i) for i in range(ends)]),
            ],
            axis=dim,
        )
    return cells


def block_product(blocks, pattern, values_in):
    stacked_count, block_count, dofs, cases = values_in.shape
    gathered = jnp.take(values_in, pattern.reshape(-1), axis=1)
    gathered = gathered.reshape(stacked_count, block_count, pattern.shape[1], dofs, cases)
    return jnp.einsum("bkij,vbkjn->vbin", blocks, gathered, precision=HIGH)


def assemble(values_in, faces):
    stacked_count, block_count, dofs, cases = values_in.shape
    flattened = values_in.reshape(stacked_count, block_count, dofs * cases)
    indicator = (faces[..., None] == jnp.arange(block_count)).astype(jnp.float32)
    face_values = jnp.einsum("fkb,vbc->fvkc", indicator, flattened, precision=HIGH)
    row_faces = extended(face_values[0:2], (("row", 0),), 1)
    col_faces = extended(face_values[2:4], (("col", 0),), 1)
    received = jnp.stack([row_faces[0], row_faces[3], col_faces[0], col_faces[3]])
    added = jnp.einsum("fkb,fvkc->vbc", indicator, received, precision=HIGH)
    return (flattened + added).reshape(values_in.shape)


def precondition(residual, weight, faces, pattern, neumann, basis, primal_map, inverse_rows):
    scaled = residual * weight
    local_term = block_product(neumann, pattern, scaled[None])[0]
    cases = residual.shape[-1]
    coarse_local = jnp.dot(basis, scaled.reshape(-1, cases), precision=HIGH)
    owned_count, coarse_total_rows = inverse_rows.shape
    indicator = (primal_map[:, None] == jnp.arange(coarse_total_rows)).astype(jnp.float32)
    owned_rhs = lax.psum_scatter(
        jnp.dot(indicator.T, coarse_local, precision=HIGH), "col", scatter_dimension=0, tiled=True
    )
    owned_rhs = lax.psum(owned_rhs, "row")
    columns = inverse_rows
    owned_solution = jnp.dot(
        columns, lax.all_gather(owned_rhs, "col", axis=0, tiled=True), precision=HIGH
    )
    columns = indicator
    own_coarse = jnp.dot(
        columns, lax.all_gather(owned_solution, "col", axis=0, tiled=True), precision=HIGH
    )
    coarse_back = jnp.dot(basis.T, own_coarse, precision=HIGH).reshape(residual.shape)
    return assemble(((local_term + coarse_back) * weight)[None], faces)[0]


def per_device(
    solution,
    residual,
    prev_direction,
    prev_dot,
    face_lists,
    multiplicity,
    block_pattern,
    schur,
    neumann_inverse,
    coarse_basis,
    primal_map,
    coarse_inverse,
):
    faces = face_lists[0, 0]
    pattern = block_pattern[0, 0]
    weight = (1.0 / multiplicity[0, 0].astype(jnp.float32))[:, None, None]
    current = residual[0, 0]
    previous = prev_direction[0, 0]
    precond = precondition(
        current,
        weight,
        faces,
        pattern,
        neumann_inverse[0, 0],
        coarse_basis[0, 0],
        primal_map[0, 0],
        coarse_inverse,
    )
    local_precond_dot = jnp.sum(current * precond * weight, axis=(0, 1))
    precond_dot = lax.psum(local_precond_dot, ("row", "col"))
    direction_mix = precond_dot / prev_dot
    direction = precond + direction_mix * previous
    image = assemble(block_product(schur[0, 0], pattern, direction[None]), faces)[0]
    curvature = lax.psum(jnp.sum(direction * image * weight, axis=(0, 1)), ("row", "col"))
    step_size = precond_dot / curvature
    new_solution = solution[0, 0] + step_size * direction
    new_residual = current - step_size * image
    return (new_solution[None, None], new_residual[None, None], direction[None, None])


def solution(mesh):
    placed = (
        P("row", "col", None, None, None),
        P("row", "col", None, None, None),
        P("row", "col", None, None, None),
        P(),
        P("row", "col", None, None),
        P("row", "col", None),
        P("row", "col", None, None),
        P("row", "col", None, None, None, None),
        P("row", "col", None, None, None, None),
        P("row", "col", None, None),
        P("row", "col", None),
        P("col", None),
    )
    return jax.shard_map(
        per_device,
        mesh=mesh,
        in_specs=placed,
        out_specs=(
            P("row", "col", None, None, None),
            P("row", "col", None, None, None),
            P("row", "col", None, None, None),
        ),
        check_vma=False,
    )
```

profile of v0, /device:TPU:1, one launch (start us, length us, event | category | flops | bytes accessed | tf_op | source)
XLA Modules:
  0.0 597.9 jit_solution(11276702184320067996)
XLA Ops:
  12.5 2.3 fusion.31
  15.1 3.6 gather_fusion
  20.9 6.2 %fusion.6 = f32[1,16,128,128]{2,3,1,0:T(8,128)} fusion(f32[16,3,128,128]{3,2,1,0:T(8,128)S(1)} %bitcast.147, f32[1,1,16,3,128,128]{5,4,3,2,1,0:T(8,128)S(1)} %copy-done), kind=kOutput, calls=%fused_computation.15 | convolution fusion | flops 1207959552 | bytes 7340032 | tf_op jit(solution)/shard_map/bkij,vbkjn->vbin/dot_general | solution.py:30
  27.1 2.6 copy.44
  29.7 194.6 %reduce-scatter.2.cloned.1.call-done = f32[32,128]{1,0:T(8,128)} async-done(((f32[1024,128]{1,0:T(8,128)}), f32[32,128]{1,0:T(8,128)}) %reduce-scatter.2.cloned.1.call-update) | async-done | bytes 16400 | tf_op jit(solution)/shard_map/reduce_scatter | solution.py:52
  224.3 26.4 %psum.21 = f32[32,128]{1,0:T(8,128)S(1)} all-reduce(f32[32,128]{1,0:T(8,128)} %reduce-scatter.2.cloned.1.call-done), channel_id=1, replica_groups=mesh['row'=8,'col'=32] {'row'}, use_global_device_ids=true, to_apply=%region_1.3 | all-reduce | flops 4096 | bytes 32768 | tf_op jit(solution)/shard_map/psum | solution.py:55
  250.7 35.9 %all_gather.6 = f32[1024,128]{1,0:T(8,128)S(1)} all-gather(f32[32,128]{1,0:T(8,128)S(1)} %psum.21), channel_id=1, replica_groups=mesh['row'=8,'col'=32] {'col'}, dimensions={0}, use_global_device_ids=true | all-gather | bytes 540672 | tf_op jit(solution)/shard_map/all_gather | solution.py:58
  287.0 35.8 %all_gather.7 = f32[1024,128]{1,0:T(8,128)S(1)} all-gather(f32[32,128]{1,0:T(8,128)S(1)} %convolution_bitcast_fusion.5), channel_id=1, replica_groups=mesh['row'=8,'col'=32] {'col'}, dimensions={0}, use_global_device_ids=true | all-gather | bytes 540672 | tf_op jit(solution)/shard_map/all_gather | solution.py:62
  325.0 2.5 copy.42
  327.6 2.4 reshape.184
  329.9 3.0 convolution_bitcast_fusion.3
  333.9 27.6 %collective-permute-start = (f32[1,1,4,16384]{3,2,0,1:T(4,128)}, f32[1,1,4,16384]{3,2,0,1:T(4,128)}, u32[]{:S(2)}, u32[]{:S(2)}) collective-permute-start(f32[1,1,4,16384]{3,2,0,1:T(4,128)} %get-tuple-element.10), channel_id=1, source_target_pairs={{0,32},{32,64},{64,96},{96,128},{128,160},{160,192},{192,224},{1,3... | collective-permute-start | bytes 786440 | tf_op jit(solution)/shard_map/ppermute | solution.py:17
  361.5 3.8 collective-permute-start.1
  365.4 3.1 collective-permute-start.2
  369.7 2.5 copy.41
  372.2 2.4 squeeze.32
  374.6 2.4 reshape.183
  378.6 3.4 fusion.1
  384.5 78.4 %psum.22 = f32[128]{0:T(128)S(1)} all-reduce(f32[128]{0:T(128)S(1)} %fusion.14), channel_id=1, replica_groups=mesh['row'=8,'col'=32] {'row','col'}, use_global_device_ids=true, to_apply=%region_3.5 | all-reduce | flops 128 | bytes 1024 | tf_op jit(solution)/shard_map/psum | solution.py:98
  462.9 2.7 fusion.12
  465.5 3.6 gather_fusion.1
  469.1 2.3 bitcast_select_fusion
  472.0 6.3 %fusion.9 = f32[1,16,128,128]{2,3,1,0:T(8,128)} fusion(f32[16,3,128,128]{3,2,1,0:T(8,128)S(1)} %bitcast.146, f32[1,1,16,3,128,128]{5,4,3,2,1,0:T(8,128)S(1)} %copy-done.7), kind=kOutput, calls=%fused_computation.16 | convolution fusion | flops 1207959552 | bytes 7340032 | tf_op jit(solution)/shard_map/bkij,vbkjn->vbin/dot_general | solution.py:30
  478.3 2.5 copy.47
  480.8 2.4 reshape.224
  483.2 2.4 reshape.187
  485.6 2.4 convolution_bitcast_fusion.1
  488.1 3.7 collective-permute-start.4
  497.0 2.5 collective-permute-done.5
  501.7 4.1 collective-permute-done.7
  508.2 78.4 %psum.23 = f32[128]{0:T(128)S(1)} all-reduce(f32[128]{0:T(128)S(1)} %bitcast_reduce_fusion), channel_id=1, replica_groups=mesh['row'=8,'col'=32] {'row','col'}, use_global_device_ids=true, to_apply=%region_6.8 | all-reduce | flops 128 | bytes 1024 | tf_op jit(solution)/shard_map/psum | solution.py:102
  586.6 4.5 multiply_add_fusion
  (63 shorter events, 27.0 us)
Async XLA Ops:
  7.2 13.7 %copy-start = (f32[1,1,16,3,128,128]{5,4,3,2,1,0:T(8,128)S(1)}, f32[1,1,16,3,128,128]{5,4,3,2,1,0:T(8,128)}, u32[]{:S(2)}) copy-start(f32[1,1,16,3,128,128]{5,4,3,2,1,0:T(8,128)} %param.22) | copy-start | bytes 9437188
  7.2 3.8 copy-start.11
  7.2 217.1 %reduce-scatter.2.cloned.1.call-start = ((), (), s32[]{:S(2)}) async-start(), calls=%async_computation.1 | async-start | bytes 540672 | tf_op jit(solution)/shard_map/reduce_scatter | solution.py:52
  8.0 6.8 %copy-start.12 = (s32[1,1,16,3]{2,1,3,0:T(1,128)S(1)}, s32[1,1,16,3]{2,1,3,0:T(1,128)}, u32[]{:S(2)}) copy-start(s32[1,1,16,3]{2,1,3,0:T(1,128)} %param.20) | copy-start | bytes 580
  20.9 265.7 %copy-start.9 = (f32[32,1024]{1,0:T(8,128)S(1)}, f32[32,1024]{1,0:T(8,128)}, u32[]{:S(2)}) copy-start(f32[32,1024]{1,0:T(8,128)} %param.25) | copy-start | bytes 393220
  27.1 295.9 %copy-start.8 = (f32[1,1,8,2048]{3,2,1,0:T(8,128)S(1)}, f32[1,1,8,2048]{3,2,1,0:T(8,128)}, u32[]{:S(2)}) copy-start(f32[1,1,8,2048]{3,2,1,0:T(8,128)} %param.23) | copy-start | bytes 196612
  286.9 43.0 %copy-start.10 = (s32[1,1,4,4]{3,2,1,0:T(4,128)S(1)}, s32[1,1,4,4]{3,2,1,0:T(4,128)}, u32[]{:S(2)}) copy-start(s32[1,1,4,4]{3,2,1,0:T(4,128)} %param.18) | copy-start | bytes 196
  333.9 43.1 %collective-permute-start = (f32[1,1,4,16384]{3,2,0,1:T(4,128)}, f32[1,1,4,16384]{3,2,0,1:T(4,128)}, u32[]{:S(2)}, u32[]{:S(2)}) collective-permute-start(f32[1,1,4,16384]{3,2,0,1:T(4,128)} %get-tuple-element.10), channel_id=1, source_target_pairs={{0,32},{32,64},{64,96},{96,128},{128,160},{160,192},{192,224},{1,3... | collective-permute-start | bytes 786440 | tf_op jit(solution)/shard_map/ppermute | solution.py:17
  361.5 15.5 %collective-permute-start.1 = (f32[1,1,4,16384]{3,2,0,1:T(4,128)}, f32[1,1,4,16384]{3,2,0,1:T(4,128)}, u32[]{:S(2)}, u32[]{:S(2)}) collective-permute-start(f32[1,1,4,16384]{3,2,0,1:T(4,128)} %get-tuple-element.13), channel_id=1, source_target_pairs={{32,0},{64,32},{96,64},{128,96},{160,128},{192,160},{224,192},{33,... | collective-permute-start | bytes 786440 | tf_op jit(solution)/shard_map/ppermute | solution.py:19
  365.4 11.7 %collective-permute-start.2 = (f32[1,1,4,16384]{3,2,0,1:T(4,128)}, f32[1,1,4,16384]{3,2,0,1:T(4,128)}, u32[]{:S(2)}, u32[]{:S(2)}) collective-permute-start(f32[1,1,4,16384]{3,2,0,1:T(4,128)} %get-tuple-element.12), channel_id=1, source_target_pairs={{0,1},{1,2},{2,3},{3,4},{4,5},{5,6},{6,7},{7,8},{8,9},{9,10},{10,1... | collective-permute-start | bytes 786440 | tf_op jit(solution)/shard_map/ppermute | solution.py:17
  368.4 10.2 %collective-permute-start.3 = (f32[1,1,4,16384]{3,2,0,1:T(4,128)S(1)}, f32[1,1,4,16384]{3,2,0,1:T(4,128)}, u32[]{:S(2)}, u32[]{:S(2)}) collective-permute-start(f32[1,1,4,16384]{3,2,0,1:T(4,128)S(1)} %get-tuple-element.11), channel_id=1, source_target_pairs={{1,0},{2,1},{3,2},{4,3},{5,4},{6,5},{7,6},{8,7},{9,8},{10,9},{11,1... | collective-permute-start | bytes 786440 | tf_op jit(solution)/shard_map/ppermute | solution.py:19
  378.6 5.5 copy-start.1
  382.0 1.0 copy-start.4
  382.0 80.9 %copy-start.13 = (f32[128]{0:T(128)S(1)}, f32[128]{0:T(128)}, u32[]{:S(2)}) copy-start(f32[128]{0:T(128)} %param.17) | copy-start | bytes 1540
  383.2 1.0 copy-start.2
  469.1 2.8 copy-start.7
  485.6 20.1 %copy-start.3 = (f32[1,16,16384]{2,1,0:T(8,128)S(1)}, f32[1,16,16384]{2,1,0:T(8,128)}, u32[]{:S(2)}) copy-start(f32[1,16,16384]{2,1,0:T(8,128)} %squeeze.32) | copy-start | bytes 3145732
  485.6 20.1 %copy-start.5 = (f32[1,16,16384]{2,1,0:T(8,128)S(1)}, f32[1,16,16384]{2,1,0:T(8,128)}, u32[]{:S(2)}) copy-start(f32[1,16,16384]{2,1,0:T(8,128)} %copy-done.4) | copy-start | bytes 3145732
  485.6 20.1 %copy-start.6 = (f32[1,16,16384]{2,1,0:T(8,128)S(1)}, f32[1,16,16384]{2,1,0:T(8,128)}, u32[]{:S(2)}) copy-start(f32[1,16,16384]{2,1,0:T(8,128)} %reshape.187) | copy-start | bytes 3145732
  488.1 8.9 %collective-permute-start.4 = (f32[1,1,4,16384]{3,2,0,1:T(4,128)S(1)}, f32[1,1,4,16384]{3,2,0,1:T(4,128)S(1)}, u32[]{:S(2)}, u32[]{:S(2)}) collective-permute-start(f32[1,1,4,16384]{3,2,0,1:T(4,128)S(1)} %get-tuple-element.6), channel_id=1, source_target_pairs={{0,32},{32,64},{64,96},{96,128},{128,160},{160,192},{192,224},{1,3... | collective-permute-start | bytes 786440 | tf_op jit(solution)/shard_map/ppermute | solution.py:17
  491.8 7.7 %collective-permute-start.5 = (f32[1,1,4,16384]{3,2,0,1:T(4,128)S(1)}, f32[1,1,4,16384]{3,2,0,1:T(4,128)S(1)}, u32[]{:S(2)}, u32[]{:S(2)}) collective-permute-start(f32[1,1,4,16384]{3,2,0,1:T(4,128)S(1)} %get-tuple-element.9), channel_id=1, source_target_pairs={{32,0},{64,32},{96,64},{128,96},{160,128},{192,160},{224,192},{33,... | collective-permute-start | bytes 786440 | tf_op jit(solution)/shard_map/ppermute | solution.py:19
  493.7 7.9 %collective-permute-start.6 = (f32[1,1,4,16384]{3,2,0,1:T(4,128)S(1)}, f32[1,1,4,16384]{3,2,0,1:T(4,128)S(1)}, u32[]{:S(2)}, u32[]{:S(2)}) collective-permute-start(f32[1,1,4,16384]{3,2,0,1:T(4,128)S(1)} %get-tuple-element.8), channel_id=1, source_target_pairs={{0,1},{1,2},{2,3},{3,4},{4,5},{5,6},{6,7},{7,8},{8,9},{9,10},{10,1... | collective-permute-start | bytes 786440 | tf_op jit(solution)/shard_map/ppermute | solution.py:17
  495.7 10.1 %collective-permute-start.7 = (f32[1,1,4,16384]{3,2,0,1:T(4,128)S(1)}, f32[1,1,4,16384]{3,2,0,1:T(4,128)S(1)}, u32[]{:S(2)}, u32[]{:S(2)}) collective-permute-start(f32[1,1,4,16384]{3,2,0,1:T(4,128)S(1)} %get-tuple-element.7), channel_id=1, source_target_pairs={{1,0},{2,1},{3,2},{4,3},{5,4},{6,5},{7,6},{8,7},{9,8},{10,9},{11,1... | collective-permute-start | bytes 786440 | tf_op jit(solution)/shard_map/ppermute | solution.py:19
Sparse Core Ops, SparseCore 0:
  12.7 211.5 reduce-scatter.1
where the time goes:
time: 599 us; the launch traced here: 598 us
  blocking collectives  255 us (43%)
  waiting for transfers between devices  205 us (34%)
  starting transfers between devices  44.6 us (7%)
  local copies, waits for them, and re-layouts  34.4 us (6%)
  matrix products  28.1 us (5%)
  other arithmetic  16.6 us (3%)
  between operations  14.3 us (2%)
    reduce_scatter x1, waiting for transfers between devices, precondition(): lax.psum_scatter(jnp.dot(indicator.T, coarse_local, precision=HIGH), 'col...  195 us
    psum x1, blocking collectives, per_device(): lax.psum(jnp.sum(direction * image * weight, axis=(0, 1)), ('row', 'col'))  78.4 us
    psum x1, blocking collectives, per_device(): precond_dot = lax.psum(local_precond_dot, ('row', 'col'))  78.4 us
    ppermute x4, starting transfers between devices, extended(): lax.ppermute(tail, axis, [(i, (i + 1) % count) for i in range(ends)])  36.3 us
    all_gather x1, blocking collectives, precondition(): lax.all_gather(owned_rhs, 'col', axis=0, tiled=True)  35.9 us
    all_gather x1, blocking collectives, precondition(): lax.all_gather(owned_solution, 'col', axis=0, tiled=True)  35.8 us
    psum x1, blocking collectives, precondition(): owned_rhs = lax.psum(owned_rhs, 'row')  26.4 us
    dot_general x2, matrix products, block_product(): return jnp.einsum('bkij,vbkjn->vbin', blocks, gathered, precision=HIGH)  12.5 us
  transfers between devices with their start and end apart: 9, of which 5 were waited for; matrix products, arithmetic and copies ran while one was open for 4% of the time, Pallas kernels for 0%

commit v1 on v0

v1 whole, which is shorter than its diff:
```python
import jax
import jax.numpy as jnp
from jax import lax
from jax.experimental import pallas as pl
from jax.experimental.pallas import tpu as pltpu
from jax.sharding import PartitionSpec as P

MESH = pl.DeviceIdType.MESH
F32 = jnp.float32
BF16 = jnp.bfloat16
ROWS, COLS = 8, 32
BLOCKS, DOFS, CASES, SLOTS, PRIMALS = 16, 128, 128, 4, 8
OWNED = 32
COARSE = OWNED * COLS
OPPOSITE = (1, 0, 3, 2)


def split(values):
    high = values.astype(BF16)
    return high, (values - high.astype(F32)).astype(BF16)


def mm(left, right):
    return jnp.dot(left, right, preferred_element_type=F32)


def wide(values):
    return jnp.concatenate(split(values), axis=1)


def iteration(
    faces, pattern, mult, pmap,
    residual_h, previous_h, solution_h, prev_dot, schur_h, neumann_h, basis_h, inverse_h,
    new_solution_h, new_residual_h, direction_h,
    nonface, sigma, place, slot_pat,
    residual, previous, solution, schur, neumann, basis, tiles, inverse,
    scaled, local, schur_hi, schur_lo, lifted, spread, chosen, picker,
    direct, direct_hl, image, out_dir, out_res,
    map_own, map_got, near_own, near_got,
    face_basis, got_basis, got_local, got_image,
    a_buf, b_own, b_got, c_buf, e_own, e_got, coarse, v_buf, w_own, w_got,
    load_sem, store_sem, send_sem, recv_sem, face_send, face_recv,
):
    i = lax.axis_index("row")
    j = lax.axis_index("col")
    row_id = lambda t: (lax.rem(i + t, ROWS), j)
    col_id = lambda t: (i, lax.rem(j + t, COLS))
    face_id = (row_id(ROWS - 1), row_id(1), col_id(COLS - 1), col_id(1))

    loads = []
    for n, (source, target) in enumerate(
        (
            (residual_h, residual), (basis_h, basis), (inverse_h, inverse), (neumann_h, neumann),
            (schur_h, schur), (previous_h, previous), (solution_h, solution),
        )
    ):
        loads.append(pltpu.make_async_copy(source, target, load_sem.at[n]))
        loads[-1].start()
    got_residual, got_basis_own, got_inverse, got_neumann, got_schur, got_previous, got_solution = loads

    barrier = pltpu.get_barrier_semaphore()

    def greet_col(t, carry):
        pl.semaphore_signal(barrier, inc=1, device_id=col_id(t), device_id_type=MESH)
        return carry

    def greet_row(t, carry):
        pl.semaphore_signal(barrier, inc=1, device_id=row_id(t), device_id_type=MESH)
        return carry

    lax.fori_loop(1, COLS, greet_col, 0)
    lax.fori_loop(1, ROWS, greet_row, 0)

    def gather_col(buffer, stage):
        def send(t, carry):
            pltpu.make_async_remote_copy(
                src_ref=buffer.at[j], dst_ref=buffer.at[j], send_sem=send_sem.at[stage], recv_sem=recv_sem.at[stage],
                device_id=col_id(t), device_id_type=MESH,
            ).start()
            return carry

        lax.fori_loop(1, COLS, send, 0)

    def scatter_row(own, got, stage, whole):
        def send(t, carry):
            source = own if whole else own.at[lax.rem(i + t, ROWS)]
            pltpu.make_async_remote_copy(
                src_ref=source, dst_ref=got.at[i], send_sem=send_sem.at[stage], recv_sem=recv_sem.at[stage],
                device_id=row_id(t), device_id_type=MESH,
            ).start()
            return carry

        lax.fori_loop(1, ROWS, send, 0)

    def await_bytes(buffer, count, sem):
        view = buffer.at[pl.ds(0, count)]
        pltpu.make_async_copy(view, view, sem).wait()

    def send_face(own, got, face, group):
        pltpu.make_async_remote_copy(
            src_ref=own, dst_ref=got.at[OPPOSITE[face]],
            send_sem=face_send.at[group, face], recv_sem=face_recv.at[group, OPPOSITE[face]],
            device_id=face_id[face], device_id_type=MESH,
        ).start()

    def find_nonface(b, count):
        on_face = faces[0, 0] == b
        for s in range(1, 16):
            on_face = jnp.logical_or(on_face, faces[s // 4, s % 4] == b)
        nonface[b] = jnp.where(on_face, -1, count)
        return count + jnp.where(on_face, 0, 1)

    lax.fori_loop(0, BLOCKS, find_nonface, jnp.int32(0))

    def find_sigma(s, count):
        named = faces[s // 4, s % 4]
        free = named >= BLOCKS
        block = jnp.int32(0)
        for b in range(BLOCKS):
            block = jnp.where(nonface[b] == count, b, block)
        sigma[s] = jnp.where(free, block, named)
        return count + jnp.where(free, 1, 0)

    lax.fori_loop(0, BLOCKS, find_sigma, jnp.int32(0))

    def find_place(b, carry):
        slot = jnp.int32(0)
        for s in range(BLOCKS):
            slot = jnp.where(sigma[s] == b, s, slot)
        place[b] = slot
        return carry

    lax.fori_loop(0, BLOCKS, find_place, 0)

    def find_slot_pat(s, carry):
        for k in range(3):
            slot_pat[s, k] = place[pattern[sigma[s], k]]
        return carry

    lax.fori_loop(0, BLOCKS, find_slot_pat, 0)

    weight = lambda b: jnp.where(mult[b] == 2, F32(0.5), F32(1.0))
    used = lambda s: jnp.where(faces[s // 4, s % 4] < BLOCKS, F32(1.0), F32(0.0))

    lanes = lax.broadcasted_iota(jnp.int32, (1, 128), 1)
    own_map = jnp.zeros((1, 128), jnp.int32)
    for p in range(PRIMALS):
        own_map = jnp.where(lax.rem(lanes, 8) == p, pmap[p], own_map)
    map_own[...] = own_map.astype(F32)
    map_got[j] = map_own[...]

    pl.semaphore_wait(barrier, COLS - 1 + ROWS - 1)

    gather_col(map_got, 0)

    got_residual.wait()
    got_basis_own.wait()

    def scale(b, carry):
        scaled[b] = wide(residual[b] * weight(b))
        return carry

    lax.fori_loop(0, BLOCKS, scale, 0, unroll=2)
    basis_hi, basis_lo = split(basis[...])
    both = mm(jnp.concatenate([basis_hi, basis_lo], axis=0), scaled[...].reshape(BLOCKS * DOFS, 2 * CASES))
    a_buf[j] = both[0:8, 0:CASES] + both[0:8, CASES:] + both[8:16, 0:CASES]
    gather_col(a_buf, 1)

    for b in range(BLOCKS):
        tiles[b] = basis[:, b * DOFS : (b + 1) * DOFS]
    for face in (2, 3, 0, 1):
        for k in range(SLOTS):
            b = sigma[face * 4 + k]
            face_basis[face, k] = tiles[b]
        send_face(face_basis.at[face], got_basis, face, 0)

    got_neumann.wait()

    def local_row(s, dot):
        b = sigma[s]
        blocks = jnp.concatenate([neumann[b, k] for k in range(3)], axis=1)
        high, low = split(blocks)
        values = jnp.concatenate([scaled[pattern[b, k]] for k in range(3)], axis=0)
        both = mm(high, values)
        row = both[:, 0:CASES] + both[:, CASES:] + mm(low, values[:, 0:CASES])
        row = row * weight(b)
        local[s // 4, lax.rem(s, 4)] = row
        return dot + jnp.sum((residual[b] * row).reshape(16, 8, CASES), axis=0)

    local_dot = lax.fori_loop(0, BLOCKS, local_row, jnp.zeros((8, CASES), F32), unroll=2)
    local_dot = jnp.sum(local_dot, axis=0, keepdims=True)
    for face in (2, 3, 0, 1):
        send_face(local.at[face], got_local, face, 1)

    await_bytes(map_got, COLS - 1, recv_sem.at[0])
    group = lanes // 8
    code = jnp.where(lax.rem(lanes, 8) == 0, F32(-1.0), F32(-2.0))
    west = map_got[lax.rem(j + COLS - 1, COLS)]
    east = map_got[lax.rem(j + 1, COLS)]
    quarter = lax.rem(group, 4)
    near_own[...] = jnp.where(quarter == 0, map_got[j], jnp.where(quarter == 1, west, jnp.where(quarter == 2, east, code)))
    near_got[i] = near_own[...]
    scatter_row(near_own, near_got, 2, True)
    halves = []
    for half in range(2):
        line = jnp.zeros((1, 128), F32)
        for t in range(16):
            line = jnp.where(group == t, map_got[half * 16 + t], line)
        halves.append(line.astype(jnp.int32))
    entries = jnp.concatenate(halves, axis=1)
    got_inverse.wait()

    def pick(c, total):
        rows = lax.broadcasted_iota(jnp.int32, (256, 256), 0) + c * 256
        hot = jnp.where(rows == entries, F32(1.0), F32(0.0)).astype(BF16)
        return total + mm(wide_rows(inverse[:, pl.ds(pl.multiple_of(c * 256, 256), 256)]), hot)

    wide_rows = lambda values: jnp.concatenate(split(values), axis=0)
    total = lax.fori_loop(0, COARSE // 256, pick, jnp.zeros((2 * OWNED, 256), F32))
    columns_hi, columns_lo = split(total[0:OWNED] + total[OWNED:])
    rows = lax.broadcasted_iota(jnp.int32, (64, OWNED), 0)
    cols = lax.broadcasted_iota(jnp.int32, (64, OWNED), 1)
    spot = (rows // 8) * 4 + lax.rem(rows, 4)
    first = lax.rem(rows, 8) < 4
    order = jnp.where(jnp.logical_and(first, spot == cols), F32(1.0), F32(0.0)).astype(BF16)
    rows = lax.broadcasted_iota(jnp.int32, (64, 256), 0)
    spot = (rows // 8) * 4 + lax.rem(rows, 4) + j * OWNED
    first = lax.rem(rows, 8) < 4
    own_hot = jnp.where(jnp.logical_and(jnp.logical_not(first), spot == entries), F32(1.0), F32(0.0))
    chosen[0:64] = (mm(order, columns_hi) + own_hot).astype(BF16)
    chosen[64:128] = mm(order, columns_lo).astype(BF16)

    await_bytes(a_buf, COLS - 1, recv_sem.at[1])
    both = mm(chosen[...], wide(a_buf[...].reshape(COLS * PRIMALS, CASES)))
    parts = both[0:64, 0:CASES] + both[0:64, CASES:] + both[64:128, 0:CASES]
    b_own[...] = parts.reshape(ROWS, 8, CASES)
    b_got[i] = b_own[i]
    scatter_row(b_own, b_got, 3, False)

    await_bytes(near_got, ROWS - 1, recv_sem.at[2])
    for half in range(2):
        line = jnp.zeros((1, 128), F32)
        for t in range(4):
            line = jnp.where(lanes // 32 == t, near_got[half * 4 + t], line)
        line = line.astype(jnp.int32)
        here = jnp.logical_and(line >= 0, lax.rem(line // 4, 8) == i)
        where_at = jnp.where(here, (line // OWNED) * 8 + lax.rem(line, 4), -1)
        for quarter_rows in range(2):
            rows = lax.broadcasted_iota(jnp.int32, (128, 128), 0) + quarter_rows * 128
            hit = jnp.logical_or(rows == where_at, jnp.logical_and(line == -1, lax.rem(rows, 8) == 4))
            hot = jnp.where(hit, F32(1.0), F32(0.0))
            picker[pl.ds(half * 128, 128), pl.ds(quarter_rows * 128, 128)] = jnp.transpose(hot).astype(BF16)

    await_bytes(b_got, ROWS - 1, recv_sem.at[3])
    held = jnp.sum(b_got[...], axis=0)
    dot = 0.5 * jnp.sum(held * pltpu.roll(held, 4, 0), axis=0, keepdims=True) + local_dot
    rows = lax.broadcasted_iota(jnp.int32, (8, CASES), 0)
    c_buf[j] = jnp.where(rows < 4, held, jnp.where(rows == 4, jnp.broadcast_to(dot, (8, CASES)), F32(0.0)))
    gather_col(c_buf, 4)

    got_schur.wait()

    def order_schur(s, carry):
        b = sigma[s]
        high, low = split(jnp.concatenate([schur[b, k] for k in range(3)], axis=1))
        schur_hi[s] = high
        schur_lo[s] = low
        return carry

    lax.fori_loop(0, BLOCKS, order_schur, 0)

    for face in range(4):
        await_bytes(got_basis.at[face], SLOTS, face_recv.at[0, face])

    def lift(s, carry):
        b = sigma[s]
        own = tiles[b]
        other = got_basis[s // 4, lax.rem(s, 4)] * used(s)
        stack = jnp.concatenate([own, other], axis=0) * weight(b)
        high, low = split(stack)
        high = high.astype(F32)
        full = jnp.concatenate([high, high, low.astype(F32), jnp.zeros((80, DOFS), F32)], axis=0)
        lifted[s] = jnp.transpose(full).astype(BF16)
        return carry

    lax.fori_loop(0, BLOCKS, lift, 0)

    for face in range(4):
        await_bytes(got_local.at[face], SLOTS, face_recv.at[1, face])
        await_bytes(local.at[face], SLOTS, face_send.at[1, face])

    def add_faces(s, carry):
        local[s // 4, lax.rem(s, 4)] = local[s // 4, lax.rem(s, 4)] + used(s) * got_local[s // 4, lax.rem(s, 4)]
        return carry

    lax.fori_loop(0, BLOCKS, add_faces, 0)
    got_previous.wait()

    await_bytes(c_buf, COLS - 1, recv_sem.at[4])
    both = mm(picker[...], wide(c_buf[...].reshape(COLS * 8, CASES)))
    spread[...] = (both[:, 0:CASES] + both[:, CASES:]).reshape(ROWS, 32, CASES)
    for t in range(ROWS):
        e_own[t, 0:8] = spread[t, 0:8]
        e_own[t, 8:16] = spread[(t + 7) % ROWS, 0:8]
        e_own[t, 16:24] = spread[(t + 1) % ROWS, 0:8]
        e_own[t, 24:48] = spread[t, 8:32]
    e_got[i] = e_own[i]
    scatter_row(e_own, e_got, 5, False)
    await_bytes(e_got, ROWS - 1, recv_sem.at[5])
    coarse[...] = jnp.sum(e_got[...], axis=0)
    precond_dot = coarse[40:41]
    mix = precond_dot / prev_dot[...]

    for face in range(4):
        stack = jnp.concatenate([coarse[0:8], coarse[8 + 8 * face : 16 + 8 * face]], axis=0)
        high, low = split(stack)
        high = high.astype(F32)
        right = jnp.concatenate([high, low.astype(F32), high, jnp.zeros((80, CASES), F32)], axis=0).astype(BF16)
        for k in range(SLOTS):
            s = face * 4 + k
            value = local[face, k] + mm(lifted[s], right) + mix * previous[sigma[s]]
            direct[s] = value
            direct_hl[s] = wide(value)

    total = jnp.zeros((8, CASES), F32)
    for face in (2, 3, 0, 1):
        def image_row(k, total):
            s = face * 4 + k
            values = jnp.concatenate([direct_hl[slot_pat[s, n]] for n in range(3)], axis=0)
            both = mm(schur_hi[s], values)
            row = both[:, 0:CASES] + both[:, CASES:] + mm(schur_lo[s], values[:, 0:CASES])
            image[face, k] = row
            return total + jnp.sum((direct[s] * row).reshape(16, 8, CASES), axis=0)

        total = lax.fori_loop(0, SLOTS, image_row, total, unroll=2)
        send_face(image.at[face], got_image, face, 2)

    v_buf[j] = jnp.sum(total, axis=0, keepdims=True)
    gather_col(v_buf, 6)

    def order_direction(b, carry):
        out_dir[b] = direct[place[b]]
        return carry

    lax.fori_loop(0, BLOCKS, order_direction, 0)
    store_direction = pltpu.make_async_copy(out_dir, direction_h, store_sem.at[0])
    store_direction.start()
    got_solution.wait()

    await_bytes(v_buf, COLS - 1, recv_sem.at[6])
    w_own[...] = jnp.sum(v_buf[...], axis=0)
    w_got[i] = w_own[...]
    scatter_row(w_own, w_got, 7, True)
    await_bytes(w_got, ROWS - 1, recv_sem.at[7])
    step_size = precond_dot / jnp.sum(w_got[...], axis=0)

    def move(b, carry):
        solution[b] = solution[b] + step_size * out_dir[b]
        return carry

    lax.fori_loop(0, BLOCKS, move, 0)
    store_solution = pltpu.make_async_copy(solution, new_solution_h, store_sem.at[1])
    store_solution.start()

    for face in range(4):
        await_bytes(got_image.at[face], SLOTS, face_recv.at[2, face])

    def finish(b, carry):
        s = place[b]
        full = image[s // 4, lax.rem(s, 4)] + used(s) * got_image[s // 4, lax.rem(s, 4)]
        out_res[b] = residual[b] - step_size * full
        return carry

    lax.fori_loop(0, BLOCKS, finish, 0)
    store_residual = pltpu.make_async_copy(out_res, new_residual_h, store_sem.at[2])
    store_residual.start()

    for buffer, stage in ((map_got, 0), (a_buf, 1), (c_buf, 4), (v_buf, 6)):
        await_bytes(buffer, COLS - 1, send_sem.at[stage])
    for buffer, stage in ((near_got, 2), (b_got, 3), (e_got, 5), (w_got, 7)):
        await_bytes(buffer, ROWS - 1, send_sem.at[stage])
    for face in range(4):
        await_bytes(face_basis.at[face], SLOTS, face_send.at[0, face])
        await_bytes(image.at[face], SLOTS, face_send.at[2, face])
    store_direction.wait()
    store_solution.wait()
    store_residual.wait()


def per_device(
    solution, residual, prev_direction, prev_dot, face_lists, multiplicity, block_pattern,
    schur, neumann_inverse, coarse_basis, primal_map, coarse_inverse,
):
    field = jax.ShapeDtypeStruct((BLOCKS, DOFS, CASES), F32)
    smem = pl.BlockSpec(memory_space=pltpu.SMEM)
    hbm = pl.BlockSpec(memory_space=pl.ANY)
    vmem = pl.BlockSpec(memory_space=pltpu.VMEM)
    V = pltpu.VMEM
    tall = (4, SLOTS, DOFS, CASES)
    outs = pl.pallas_call(
        iteration,
        out_shape=(field, field, field),
        in_specs=[smem] * 4 + [hbm] * 3 + [vmem] + [hbm] * 4,
        out_specs=(hbm, hbm, hbm),
        scratch_shapes=[
            pltpu.SMEM((16,), jnp.int32), pltpu.SMEM((16,), jnp.int32), pltpu.SMEM((16,), jnp.int32),
            pltpu.SMEM((16, 3), jnp.int32),
            V((16, 128, 128), F32), V((16, 128, 128), F32), V((16, 128, 128), F32),
            V((16, 3, 128, 128), F32), V((16, 3, 128, 128), F32), V((8, 2048), F32), V((16, 8, 128), F32), V((32, 1024), F32),
            V((16, 128, 256), BF16), V(tall, F32), V((16, 128, 384), BF16), V((16, 128, 384), BF16),
            V((16, 128, 128), BF16), V((8, 32, 128), F32), V((128, 256), BF16), V((256, 256), BF16),
            V((16, 128, 128), F32), V((16, 128, 256), BF16), V(tall, F32), V((16, 128, 128), F32), V((16, 128, 128), F32),
            V((1, 128), F32), V((32, 1, 128), F32), V((1, 128), F32), V((8, 1, 128), F32),
            V((4, 4, 8, 128), F32), V((4, 4, 8, 128), F32), V(tall, F32), V(tall, F32),
            V((32, 8, 128), F32), V((8, 8, 128), F32), V((8, 8, 128), F32), V((32, 8, 128), F32),
            V((8, 48, 128), F32), V((8, 48, 128), F32), V((48, 128), F32), V((32, 1, 128), F32),
            V((1, 128), F32), V((8, 1, 128), F32),
            pltpu.SemaphoreType.DMA((7,)), pltpu.SemaphoreType.DMA((3,)), pltpu.SemaphoreType.DMA((8,)),
            pltpu.SemaphoreType.DMA((8,)), pltpu.SemaphoreType.DMA((3, 4)), pltpu.SemaphoreType.DMA((3, 4)),
        ],
        compiler_params=pltpu.CompilerParams(
            collective_id=0, has_side_effects=True, vmem_limit_bytes=48 * 1024 * 1024
        ),
        name="iteration",
    )(
        face_lists[0, 0], block_pattern[0, 0], multiplicity[0, 0], primal_map[0, 0],
        residual[0, 0], prev_direction[0, 0], solution[0, 0], prev_dot.reshape(1, CASES),
        schur[0, 0], neumann_inverse[0, 0], coarse_basis[0, 0], coarse_inverse,
    )
    return tuple(out[None, None] for out in outs)


def solution(mesh):
    field = P("row", "col", None, None, None)
    return jax.shard_map(
        per_device,
        mesh=mesh,
        in_specs=(
            field, field, field, P(), P("row", "col", None, None), P("row", "col", None), P("row", "col", None, None),
            P("row", "col", None, None, None, None), P("row", "col", None, None, None, None),
            P("row", "col", None, None), P("row", "col", None), P("col", None),
        ),
        out_specs=(field, field, field),
        check_vma=False,
    )
```

time: 599 us -> 63.2 us (0.11)
  blocking collectives: 255 us -> 0 us
  waiting for transfers between devices: 205 us -> 0 us
  Pallas kernels: 0 us -> 51.7 us
  starting transfers between devices: 44.6 us -> 0 us
  matrix products: 28.1 us -> 0 us
  local copies, waits for them, and re-layouts: 34.4 us -> 10.5 us
  other arithmetic: 16.6 us -> 0 us
  between operations: 14.3 us -> 0.65 us
    reduce_scatter x1 -> x0, waiting for transfers between devices: 195 us -> none  [precondition(): lax.psum_scatter(jnp.dot(indicator.T, coarse_local, precision=HIGH), 'col...]
    psum x3 -> x0, blocking collectives: 183 us -> none  [the longest x1 78.4 us: per_device(): lax.psum(jnp.sum(direction * image * weight, axis=(0, 1)), ('row', 'col'))]
    all_gather x2 -> x0, blocking collectives: 71.6 us -> none  [the longest x1 35.9 us: precondition(): lax.all_gather(owned_rhs, 'col', axis=0, tiled=True)]
    pallas_call x0 -> x1, Pallas kernels: none -> 51.7 us  [per_device(): pl.pallas_call(iteration, out_shape=(field, field, field), in_specs=[smem...]
    ppermute x8 -> x0, starting transfers between devices: 44.6 us -> none  [the longest x4 36.3 us: extended(): lax.ppermute(tail, axis, [(i, (i + 1) % count) for i in range(ends)])]
    dot_general x11 -> x0, matrix products: 28.1 us -> none  [the longest x2 12.5 us: block_product(): return jnp.einsum('bkij,vbkjn->vbin', blocks, gathered, precision=HIGH)]
    ppermute x8 -> x0, waiting for transfers between devices: 10.4 us -> none  [the longest x4 8.2 us: extended(): lax.ppermute(head, axis, [((i + 1) % count, i) for i in range(ends)])]
    transpose x3 -> x0, local copies, waits for them, and re-layouts: 7.62 us -> none  [block_product(): return jnp.einsum('bkij,vbkjn->vbin', blocks, gathered, precision=HIGH)]
  transfers between devices with their start and end apart: 9 -> 0, of which waited for: 5 -> 0; matrix products, arithmetic and copies ran while one was open for 4% -> 0% of each run, Pallas kernels for 0% -> 0%
where the time goes in v1:
time: 63.2 us; the launch traced here: 62.9 us
  Pallas kernels  51.7 us (82%)
  local copies, waits for them, and re-layouts  10.5 us (17%)
  between operations  0.65 us (1%)
    pallas_call x1, Pallas kernels, per_device(): pl.pallas_call(iteration, out_shape=(field, field, field), in_specs=[smem...  51.7 us
    unnamed x19, local copies, waits for them, and re-layouts  9.75 us

profile of v1, /device:TPU:1, one launch (start us, length us, event | category | flops | bytes accessed | tf_op | source)
XLA Modules:
  0.0 62.9 jit_solution(4770591344385144205)
XLA Ops:
  0.6 0.8 %copy.16 = s32[1,1,16,3]{3,2,1,0:T(8,128)S(1)} copy(s32[1,1,16,3]{2,1,3,0:T(1,128)} %param.18) | data formatting | bytes 384 | tf_op jit(solution)/shard_map/squeeze | solution.py:426
  1.4 0.0 copy-start
  1.4 1.2 %copy-done = f32[1,1,16,128,128]{4,3,2,1,0:T(8,128)S(1)} copy-done((f32[1,1,16,128,128]{4,3,2,1,0:T(8,128)S(1)}, f32[1,1,16,128,128]{4,3,2,1,0:T(8,128)}, u32[]{:S(2)}) %copy-start) | copy-done | bytes 1048600
  2.6 0.0 copy-start.1
  2.6 1.2 %copy-done.1 = f32[1,1,16,128,128]{4,3,2,1,0:T(8,128)S(1)} copy-done((f32[1,1,16,128,128]{4,3,2,1,0:T(8,128)S(1)}, f32[1,1,16,128,128]{4,3,2,1,0:T(8,128)}, u32[]{:S(2)}) %copy-start.1) | copy-done | bytes 1048600
  3.8 0.0 copy-start.2
  3.8 0.9 %copy-done.2 = f32[32,1024]{1,0:T(8,128)S(1)} copy-done((f32[32,1024]{1,0:T(8,128)S(1)}, f32[32,1024]{1,0:T(8,128)}, u32[]{:S(2)}) %copy-start.2) | copy-done | bytes 131096
  4.7 0.0 copy-start.3
  4.7 0.8 %copy-done.3 = f32[1,1,8,2048]{3,2,1,0:T(8,128)S(1)} copy-done((f32[1,1,8,2048]{3,2,1,0:T(8,128)S(1)}, f32[1,1,8,2048]{3,2,1,0:T(8,128)}, u32[]{:S(2)}) %copy-start.3) | copy-done | bytes 65560
  5.6 0.0 copy-start.4
  5.6 0.7 %copy-done.4 = s32[1,1,4,4]{3,2,1,0:T(4,128)S(1)} copy-done((s32[1,1,4,4]{3,2,1,0:T(4,128)S(1)}, s32[1,1,4,4]{3,2,1,0:T(4,128)}, u32[]{:S(2)}) %copy-start.4) | copy-done | bytes 88
  6.3 0.0 copy-start.5
  6.3 0.7 %copy-done.5 = s32[1,1,16]{2,1,0:T(1,128)S(1)} copy-done((s32[1,1,16]{2,1,0:T(1,128)S(1)}, s32[1,1,16]{2,1,0:T(1,128)}, u32[]{:S(2)}) %copy-start.5) | copy-done | bytes 88
  6.9 0.0 copy-start.6
  6.9 0.7 %copy-done.6 = s32[1,1,8]{2,1,0:T(1,128)S(1)} copy-done((s32[1,1,8]{2,1,0:T(1,128)S(1)}, s32[1,1,8]{2,1,0:T(1,128)}, u32[]{:S(2)}) %copy-start.6) | copy-done | bytes 56
  7.6 0.0 copy-start.7
  7.6 0.7 %copy-done.7 = f32[128]{0:T(128)S(1)} copy-done((f32[128]{0:T(128)S(1)}, f32[128]{0:T(128)}, u32[]{:S(2)}) %copy-start.7) | copy-done | bytes 536
  8.2 51.7 %iteration.1 = (f32[16,128,128]{2,1,0:T(8,128)S(1)}, f32[16,128,128]{2,1,0:T(8,128)S(1)}, f32[16,128,128]{2,1,0:T(8,128)S(1)}) custom-call(s32[4,4]{1,0:T(4,128)S(1)} %bitcast.21, s32[16,3]{1,0:T(8,128)S(1)} %bitcast.20, s32[16]{0:T(128)S(1)} %bitcast.22, s32[8]{0:T(128)S(1)} %bitcast.23, f32[16,128,128]{2,1,0:T(8,128)S(1)} %bitcast.14, ...), custom_call_target="tpu_custom_call" | custom-call | tf_op jit(solution)/shard_map/iteration/pallas_call | solution.py:400
  60.0 1.0 %copy.20 = f32[1,1,16,128,128]{4,3,2,1,0:T(8,128)} copy(f32[1,1,16,128,128]{4,3,2,1,0:T(8,128)S(1)} %bitcast.18) | data formatting | bytes 2097152
  60.9 1.0 %copy.21 = f32[1,1,16,128,128]{4,3,2,1,0:T(8,128)} copy(f32[1,1,16,128,128]{4,3,2,1,0:T(8,128)S(1)} %bitcast.17) | data formatting | bytes 2097152
  61.9 1.0 %copy.22 = f32[1,1,16,128,128]{4,3,2,1,0:T(8,128)} copy(f32[1,1,16,128,128]{4,3,2,1,0:T(8,128)S(1)} %bitcast.16) | data formatting | bytes 2097152
Async XLA Ops:
  1.4 1.2 %copy-start = (f32[1,1,16,128,128]{4,3,2,1,0:T(8,128)S(1)}, f32[1,1,16,128,128]{4,3,2,1,0:T(8,128)}, u32[]{:S(2)}) copy-start(f32[1,1,16,128,128]{4,3,2,1,0:T(8,128)} %param.13) | copy-start | bytes 3145732
  2.6 1.2 %copy-start.1 = (f32[1,1,16,128,128]{4,3,2,1,0:T(8,128)S(1)}, f32[1,1,16,128,128]{4,3,2,1,0:T(8,128)}, u32[]{:S(2)}) copy-start(f32[1,1,16,128,128]{4,3,2,1,0:T(8,128)} %param.14) | copy-start | bytes 3145732
  3.8 0.9 %copy-start.2 = (f32[32,1024]{1,0:T(8,128)S(1)}, f32[32,1024]{1,0:T(8,128)}, u32[]{:S(2)}) copy-start(f32[32,1024]{1,0:T(8,128)} %inverse_h.1) | copy-start | bytes 393220
  4.7 0.8 %copy-start.3 = (f32[1,1,8,2048]{3,2,1,0:T(8,128)S(1)}, f32[1,1,8,2048]{3,2,1,0:T(8,128)}, u32[]{:S(2)}) copy-start(f32[1,1,8,2048]{3,2,1,0:T(8,128)} %param.21) | copy-start | bytes 196612
  5.6 0.7 %copy-start.4 = (s32[1,1,4,4]{3,2,1,0:T(4,128)S(1)}, s32[1,1,4,4]{3,2,1,0:T(4,128)}, u32[]{:S(2)}) copy-start(s32[1,1,4,4]{3,2,1,0:T(4,128)} %param.16) | copy-start | bytes 196
  6.3 0.7 %copy-start.5 = (s32[1,1,16]{2,1,0:T(1,128)S(1)}, s32[1,1,16]{2,1,0:T(1,128)}, u32[]{:S(2)}) copy-start(s32[1,1,16]{2,1,0:T(1,128)} %param.17) | copy-start | bytes 196
  6.9 0.7 %copy-start.6 = (s32[1,1,8]{2,1,0:T(1,128)S(1)}, s32[1,1,8]{2,1,0:T(1,128)}, u32[]{:S(2)}) copy-start(s32[1,1,8]{2,1,0:T(1,128)} %param.22) | copy-start | bytes 100
  7.6 0.7 %copy-start.7 = (f32[128]{0:T(128)S(1)}, f32[128]{0:T(128)}, u32[]{:S(2)}) copy-start(f32[128]{0:T(128)} %param.15) | copy-start | bytes 1540

commit v2 on v1

v2 whole, which is shorter than its diff:
```python
import jax
import jax.numpy as jnp
from jax import lax
from jax.experimental import pallas as pl
from jax.experimental.pallas import tpu as pltpu
from jax.sharding import PartitionSpec as P

MESH = pl.DeviceIdType.MESH
F32 = jnp.float32
BF16 = jnp.bfloat16
ROWS, COLS = 8, 32
BLOCKS, DOFS, CASES, SLOTS, PRIMALS = 16, 128, 128, 4, 8
OWNED = 32
COARSE = OWNED * COLS
OPPOSITE = (1, 0, 3, 2)


def split(values):
    high = values.astype(BF16)
    return high, (values - high.astype(F32)).astype(BF16)


def mm(left, right):
    return jnp.dot(left, right, preferred_element_type=F32)


def wide(values):
    return jnp.concatenate(split(values), axis=1)


def iteration(
    faces_h, pattern_h, mult_h, pmap_h, prev_dot_h,
    residual_h, previous_h, solution_h, schur_h, neumann_h, basis_h, inverse_h,
    new_solution, out_res, out_dir,
    faces, pattern, mult, pmap, prev_dot,
    nonface, sigma, place, slot_pat,
    residual, previous, solution, schur, neumann, basis, tiles, inverse,
    scaled, local, schur_hi, schur_lo, lifted, spread, chosen, picker,
    direct, direct_hl, image,
    map_got, near_own, near_got,
    face_basis, got_basis, got_local, got_image,
    a_buf, b_own, b_got, c_buf, e_own, e_got, coarse, v_buf, w_own, w_got,
    load_sem, send_sem, recv_sem, face_send, face_recv,
):
    i = lax.axis_index("row")
    j = lax.axis_index("col")
    z, x = j // 4, lax.rem(j, 4)
    row_id = lambda t: (lax.rem(i + t, ROWS), j)
    col_id = lambda t: (i, lax.rem(j + t, COLS))
    face_id = (row_id(ROWS - 1), row_id(1), col_id(COLS - 1), col_id(1))
    z_at = [lax.rem(z + t, 8) * 4 for t in range(8)]
    x_at = [lax.rem(x + t, 4) for t in range(4)]
    z_far, x_far = (4, 3, 5, 2, 6, 1, 7), (2, 1, 3)
    z_ids = [(i, z_at[t] + x) for t in z_far]
    x_ids = [(i, z * 4 + x_at[t]) for t in x_far]
    hops = lambda t: min(t[0], 8 - t[0]) + min(t[1], 4 - t[1])
    offsets = sorted(((dz, dx) for dz in range(8) for dx in range(4) if dz or dx), key=lambda t: -hops(t))
    col_ids = [(i, z_at[dz] + x_at[dx]) for dz, dx in offsets]
    row_ids = [row_id(t) for t in (4, 5, 3, 6, 2, 7, 1)]

    pairs = (
        (faces_h, faces), (pattern_h, pattern), (mult_h, mult), (pmap_h, pmap),
        (residual_h, residual), (basis_h, basis), (inverse_h, inverse), (neumann_h, neumann),
        (schur_h, schur), (previous_h, previous), (solution_h, solution), (prev_dot_h, prev_dot),
    )
    loads = [pltpu.make_async_copy(source, target, load_sem.at[n]) for n, (source, target) in enumerate(pairs)]
    for n in range(6):
        loads[n].start()

    barrier = pltpu.get_barrier_semaphore()
    for peer in z_ids + x_ids + row_ids:
        pl.semaphore_signal(barrier, inc=1, device_id=peer, device_id_type=MESH)
    loads[7].start()
    loads[6].start()

    def push(source, target, peers, stage):
        for peer in peers:
            pltpu.make_async_remote_copy(
                src_ref=source, dst_ref=target, send_sem=send_sem.at[stage], recv_sem=recv_sem.at[stage],
                device_id=peer, device_id_type=MESH,
            ).start()

    def scatter_row(own, got, stage):
        for t in (4, 5, 3, 6, 2, 7, 1):
            pltpu.make_async_remote_copy(
                src_ref=own.at[lax.rem(i + t, ROWS)], dst_ref=got.at[i],
                send_sem=send_sem.at[stage], recv_sem=recv_sem.at[stage],
                device_id=row_id(t), device_id_type=MESH,
            ).start()

    def await_bytes(buffer, count, sem):
        view = buffer.at[pl.ds(0, count)]
        pltpu.make_async_copy(view, view, sem).wait()

    def send_face(own, got, face, group):
        pltpu.make_async_remote_copy(
            src_ref=own, dst_ref=got.at[OPPOSITE[face]],
            send_sem=face_send.at[group, face], recv_sem=face_recv.at[group, OPPOSITE[face]],
            device_id=face_id[face], device_id_type=MESH,
        ).start()

    for n in (2, 3):
        loads[n].wait()
    weight = lambda b: jnp.where(mult[0, b] == 2, F32(0.5), F32(1.0))
    used = lambda s: jnp.where(faces[s // 4, s % 4] < BLOCKS, F32(1.0), F32(0.0))

    lanes = lax.broadcasted_iota(jnp.int32, (1, 128), 1)
    own_map = jnp.zeros((1, 128), jnp.int32)
    for p in range(PRIMALS):
        own_map = jnp.where(lax.rem(lanes, 8) == p, pmap[0, p], own_map)
    home = x * 8 + z
    map_got[home] = own_map.astype(F32)

    loads[4].wait()
    loads[5].wait()

    both = jnp.zeros((16, 2 * CASES), F32)
    for b in range(0, BLOCKS, 2):
        for n in (b, b + 1):
            scaled[n] = wide(residual[n] * weight(n))
        left = jnp.concatenate(split(basis[:, b * DOFS : (b + 2) * DOFS]), axis=0)
        both = both + mm(left, scaled[pl.ds(b, 2)].reshape(2 * DOFS, 2 * CASES))
    a_buf[home] = both[0:8, 0:CASES] + both[0:8, CASES:] + both[8:16, 0:CASES]

    pl.semaphore_wait(barrier, 17)
    push(map_got.at[home], map_got.at[home], z_ids, 0)
    push(a_buf.at[home], a_buf.at[home], z_ids, 1)
    for n in (8, 9, 10, 11):
        loads[n].start()

    for n in (0, 1):
        loads[n].wait()

    def find_nonface(b, count):
        on_face = faces[0, 0] == b
        for s in range(1, 16):
            on_face = jnp.logical_or(on_face, faces[s // 4, s % 4] == b)
        nonface[b] = jnp.where(on_face, -1, count)
        return count + jnp.where(on_face, 0, 1)

    lax.fori_loop(0, BLOCKS, find_nonface, jnp.int32(0))

    def find_sigma(s, count):
        named = faces[s // 4, s % 4]
        free = named >= BLOCKS
        block = jnp.int32(0)
        for b in range(BLOCKS):
            block = jnp.where(nonface[b] == count, b, block)
        sigma[s] = jnp.where(free, block, named)
        return count + jnp.where(free, 1, 0)

    lax.fori_loop(0, BLOCKS, find_sigma, jnp.int32(0))

    def find_place(b, carry):
        slot = jnp.int32(0)
        for s in range(BLOCKS):
            slot = jnp.where(sigma[s] == b, s, slot)
        place[b] = slot
        return carry

    lax.fori_loop(0, BLOCKS, find_place, 0)

    def find_slot_pat(s, carry):
        for k in range(3):
            slot_pat[s, k] = place[pattern[k, 0, sigma[s]]]
        return carry

    lax.fori_loop(0, BLOCKS, find_slot_pat, 0)

    for b in range(BLOCKS):
        tiles[b] = basis[:, b * DOFS : (b + 1) * DOFS]
    for face in (2, 3, 0, 1):
        for k in range(SLOTS):
            b = sigma[face * 4 + k]
            face_basis[face, k] = tiles[b]

    loads[7].wait()

    def local_row(s, dot):
        b = sigma[s]
        blocks = jnp.concatenate([neumann[b, k] for k in range(3)], axis=1)
        high, low = split(blocks)
        values = jnp.concatenate([scaled[pattern[k, 0, b]] for k in range(3)], axis=0)
        both = mm(high, values)
        row = both[:, 0:CASES] + both[:, CASES:] + mm(low, values[:, 0:CASES])
        row = row * weight(b)
        local[s // 4, lax.rem(s, 4)] = row
        return dot + jnp.sum((residual[b] * row).reshape(16, 8, CASES), axis=0)

    local_dot = lax.fori_loop(0, BLOCKS, local_row, jnp.zeros((8, CASES), F32), unroll=2)
    local_dot = jnp.sum(local_dot, axis=0, keepdims=True)
    line_of = lambda buffer: buffer.at[pl.ds(x * 8, 8)]
    await_bytes(map_got, 7, recv_sem.at[0])
    push(line_of(map_got), line_of(map_got), x_ids, 2)
    await_bytes(a_buf, 7, recv_sem.at[1])
    push(line_of(a_buf), line_of(a_buf), x_ids, 3)
    for face in (2, 3, 0, 1):
        send_face(face_basis.at[face], got_basis, face, 0)

    await_bytes(map_got, 24, recv_sem.at[2])
    group = lanes // 8
    code = jnp.where(lax.rem(lanes, 8) == 0, F32(-1.0), F32(-2.0))
    before, after = lax.rem(j + COLS - 1, COLS), lax.rem(j + 1, COLS)
    west = map_got[lax.rem(before, 4) * 8 + before // 4]
    east = map_got[lax.rem(after, 4) * 8 + after // 4]
    quarter = lax.rem(group, 4)
    near_own[...] = jnp.where(quarter == 0, map_got[home], jnp.where(quarter == 1, west, jnp.where(quarter == 2, east, code)))
    near_got[i] = near_own[...]
    push(near_own, near_got.at[i], row_ids, 4)
    halves = []
    for half in range(2):
        line = jnp.zeros((1, 128), F32)
        for t in range(16):
            line = jnp.where(group == t, map_got[half * 16 + t], line)
        halves.append(line.astype(jnp.int32))
    entries = jnp.concatenate(halves, axis=1)
    loads[6].wait()

    def pick(c, total):
        rows = lax.broadcasted_iota(jnp.int32, (256, 256), 0) + c * 256
        hot = jnp.where(rows == entries, F32(1.0), F32(0.0)).astype(BF16)
        return total + mm(wide_rows(inverse[:, pl.ds(pl.multiple_of(c * 256, 256), 256)]), hot)

    wide_rows = lambda values: jnp.concatenate(split(values), axis=0)
    total = lax.fori_loop(0, COARSE // 256, pick, jnp.zeros((2 * OWNED, 256), F32))
    columns_hi, columns_lo = split(total[0:OWNED] + total[OWNED:])
    rows = lax.broadcasted_iota(jnp.int32, (64, OWNED), 0)
    cols = lax.broadcasted_iota(jnp.int32, (64, OWNED), 1)
    spot = (rows // 8) * 4 + lax.rem(rows, 4)
    first = lax.rem(rows, 8) < 4
    order = jnp.where(jnp.logical_and(first, spot == cols), F32(1.0), F32(0.0)).astype(BF16)
    rows = lax.broadcasted_iota(jnp.int32, (64, 256), 0)
    spot = (rows // 8) * 4 + lax.rem(rows, 4) + j * OWNED
    first = lax.rem(rows, 8) < 4
    own_hot = jnp.where(jnp.logical_and(jnp.logical_not(first), spot == entries), F32(1.0), F32(0.0))
    chosen[0:64] = (mm(order, columns_hi) + own_hot).astype(BF16)
    chosen[64:128] = mm(order, columns_lo).astype(BF16)

    await_bytes(a_buf, 24, recv_sem.at[3])
    both = mm(chosen[...], wide(a_buf[...].reshape(COLS * PRIMALS, CASES)))
    parts = both[0:64, 0:CASES] + both[0:64, CASES:] + both[64:128, 0:CASES]
    b_own[...] = parts.reshape(ROWS, 8, CASES)
    b_got[i] = b_own[i]
    scatter_row(b_own, b_got, 5)

    await_bytes(near_got, ROWS - 1, recv_sem.at[4])
    for half in range(2):
        line = jnp.zeros((1, 128), F32)
        for t in range(4):
            line = jnp.where(lanes // 32 == t, near_got[half * 4 + t], line)
        line = line.astype(jnp.int32)
        here = jnp.logical_and(line >= 0, lax.rem(line // 4, 8) == i)
        where_at = jnp.where(here, (line // OWNED) * 8 + lax.rem(line, 4), -1)
        for quarter_rows in range(2):
            rows = lax.broadcasted_iota(jnp.int32, (128, 128), 0) + quarter_rows * 128
            hit = jnp.logical_or(rows == where_at, jnp.logical_and(line == -1, lax.rem(rows, 8) == 4))
            hot = jnp.where(hit, F32(1.0), F32(0.0))
            picker[pl.ds(half * 128, 128), pl.ds(quarter_rows * 128, 128)] = jnp.transpose(hot).astype(BF16)

    await_bytes(b_got, ROWS - 1, recv_sem.at[5])
    held = jnp.sum(b_got[...], axis=0)
    dot = 0.5 * jnp.sum(held * pltpu.roll(held, 4, 0), axis=0, keepdims=True) + local_dot
    rows = lax.broadcasted_iota(jnp.int32, (8, CASES), 0)
    c_buf[j] = jnp.where(rows < 4, held, jnp.where(rows == 4, jnp.broadcast_to(dot, (8, CASES)), F32(0.0)))
    push(c_buf.at[j], c_buf.at[j], col_ids, 6)
    for face in (2, 3, 0, 1):
        send_face(local.at[face], got_local, face, 1)

    loads[8].wait()

    def order_schur(s, carry):
        b = sigma[s]
        high, low = split(jnp.concatenate([schur[b, k] for k in range(3)], axis=1))
        schur_hi[s] = high
        schur_lo[s] = low
        return carry

    lax.fori_loop(0, BLOCKS, order_schur, 0)

    for face in range(4):
        await_bytes(got_basis.at[face], SLOTS, face_recv.at[0, face])

    def lift(s, carry):
        b = sigma[s]
        own = tiles[b]
        other = got_basis[s // 4, lax.rem(s, 4)] * used(s)
        stack = jnp.concatenate([own, other], axis=0) * weight(b)
        high, low = split(stack)
        high = high.astype(F32)
        full = jnp.concatenate([high, high, low.astype(F32), jnp.zeros((80, DOFS), F32)], axis=0)
        lifted[s] = jnp.transpose(full).astype(BF16)
        return carry

    lax.fori_loop(0, BLOCKS, lift, 0)

    await_bytes(c_buf, COLS - 1, recv_sem.at[6])
    both = mm(picker[...], wide(c_buf[...].reshape(COLS * 8, CASES)))
    spread[...] = (both[:, 0:CASES] + both[:, CASES:]).reshape(ROWS, 32, CASES)
    for t in range(ROWS):
        e_own[t, 0:8] = spread[t, 0:8]
        e_own[t, 8:16] = spread[(t + 7) % ROWS, 0:8]
        e_own[t, 16:24] = spread[(t + 1) % ROWS, 0:8]
        e_own[t, 24:48] = spread[t, 8:32]
    e_got[i] = e_own[i]
    scatter_row(e_own, e_got, 7)
    for face in range(4):
        await_bytes(got_local.at[face], SLOTS, face_recv.at[1, face])
        await_bytes(local.at[face], SLOTS, face_send.at[1, face])

    def add_faces(s, carry):
        local[s // 4, lax.rem(s, 4)] = local[s // 4, lax.rem(s, 4)] + used(s) * got_local[s // 4, lax.rem(s, 4)]
        return carry

    lax.fori_loop(0, BLOCKS, add_faces, 0)
    loads[9].wait()

    await_bytes(e_got, ROWS - 1, recv_sem.at[7])
    loads[11].wait()
    coarse[...] = jnp.sum(e_got[...], axis=0)
    precond_dot = coarse[40:41]
    mix = precond_dot / prev_dot[...]

    for face in range(4):
        stack = jnp.concatenate([coarse[0:8], coarse[8 + 8 * face : 16 + 8 * face]], axis=0)
        high, low = split(stack)
        high = high.astype(F32)
        right = jnp.concatenate([high, low.astype(F32), high, jnp.zeros((80, CASES), F32)], axis=0).astype(BF16)
        for k in range(SLOTS):
            s = face * 4 + k
            value = local[face, k] + mm(lifted[s], right) + mix * previous[sigma[s]]
            direct[s] = value
            direct_hl[s] = wide(value)

    total = jnp.zeros((8, CASES), F32)
    for face in (2, 3, 0, 1):
        def image_row(k, total):
            s = face * 4 + k
            values = jnp.concatenate([direct_hl[slot_pat[s, n]] for n in range(3)], axis=0)
            both = mm(schur_hi[s], values)
            row = both[:, 0:CASES] + both[:, CASES:] + mm(schur_lo[s], values[:, 0:CASES])
            image[face, k] = row
            return total + jnp.sum((direct[s] * row).reshape(16, 8, CASES), axis=0)

        total = lax.fori_loop(0, SLOTS, image_row, total, unroll=2)

    v_buf[j] = jnp.sum(total, axis=0, keepdims=True)
    push(v_buf.at[j], v_buf.at[j], col_ids, 8)
    for face in (2, 3, 0, 1):
        send_face(image.at[face], got_image, face, 2)

    def order_direction(b, carry):
        out_dir[b] = direct[place[b]]
        return carry

    lax.fori_loop(0, BLOCKS, order_direction, 0)
    loads[10].wait()

    await_bytes(v_buf, COLS - 1, recv_sem.at[8])
    w_own[...] = jnp.sum(v_buf[...], axis=0)
    w_got[i] = w_own[...]
    push(w_own, w_got.at[i], row_ids, 9)
    await_bytes(w_got, ROWS - 1, recv_sem.at[9])
    step_size = precond_dot / jnp.sum(w_got[...], axis=0)

    def move(b, carry):
        new_solution[b] = solution[b] + step_size * out_dir[b]
        return carry

    lax.fori_loop(0, BLOCKS, move, 0)

    for face in range(4):
        await_bytes(got_image.at[face], SLOTS, face_recv.at[2, face])

    def finish(b, carry):
        s = place[b]
        full = image[s // 4, lax.rem(s, 4)] + used(s) * got_image[s // 4, lax.rem(s, 4)]
        out_res[b] = residual[b] - step_size * full
        return carry

    lax.fori_loop(0, BLOCKS, finish, 0)

    for buffer, count, stage in (
        (map_got, 7, 0), (a_buf, 7, 1), (map_got, 24, 2), (a_buf, 24, 3), (near_got, 7, 4), (b_got, 7, 5),
        (c_buf, 31, 6), (e_got, 7, 7), (v_buf, 31, 8), (w_got, 7, 9),
    ):
        await_bytes(buffer, count, send_sem.at[stage])
    for face in range(4):
        await_bytes(face_basis.at[face], SLOTS, face_send.at[0, face])
        await_bytes(image.at[face], SLOTS, face_send.at[2, face])


def deliver(a, b, c, a_out, b_out, c_out, sem):
    copies = [pltpu.make_async_copy(s, t, sem.at[n]) for n, (s, t) in enumerate(((a, a_out), (b, b_out), (c, c_out)))]
    for copy in copies:
        copy.start()
    for copy in copies:
        copy.wait()


def per_device(
    solution, residual, prev_direction, prev_dot, face_lists, multiplicity, block_pattern,
    schur, neumann_inverse, coarse_basis, primal_map, coarse_inverse,
):
    field = jax.ShapeDtypeStruct((BLOCKS, DOFS, CASES), F32)
    hbm = pl.BlockSpec(memory_space=pltpu.HBM)
    anywhere = pl.BlockSpec(memory_space=pl.ANY)
    V = pltpu.VMEM
    tall = (4, SLOTS, DOFS, CASES)
    outs = pl.pallas_call(
        iteration,
        out_shape=(pltpu.VMEM((BLOCKS, DOFS, CASES), F32),) * 3,
        in_specs=[hbm] * 12,
        out_specs=(pl.BlockSpec(memory_space=pltpu.VMEM),) * 3,
        scratch_shapes=[
            pltpu.SMEM((4, 4), jnp.int32), pltpu.SMEM((3, 1, 16), jnp.int32), pltpu.SMEM((1, 16), jnp.int32),
            pltpu.SMEM((1, 8), jnp.int32), V((1, 128), F32),
            pltpu.SMEM((16,), jnp.int32), pltpu.SMEM((16,), jnp.int32), pltpu.SMEM((16,), jnp.int32),
            pltpu.SMEM((16, 3), jnp.int32),
            V((16, 128, 128), F32), V((16, 128, 128), F32), V((16, 128, 128), F32),
            V((16, 3, 128, 128), F32), V((16, 3, 128, 128), F32), V((8, 2048), F32), V((16, 8, 128), F32), V((32, 1024), F32),
            V((16, 128, 256), BF16), V(tall, F32), V((16, 128, 384), BF16), V((16, 128, 384), BF16),
            V((16, 128, 128), BF16), V((8, 32, 128), F32), V((128, 256), BF16), V((256, 256), BF16),
            V((16, 128, 128), F32), V((16, 128, 256), BF16), V(tall, F32),
            V((32, 1, 128), F32), V((1, 128), F32), V((8, 1, 128), F32),
            V((4, 4, 8, 128), F32), V((4, 4, 8, 128), F32), V(tall, F32), V(tall, F32),
            V((32, 8, 128), F32), V((8, 8, 128), F32), V((8, 8, 128), F32), V((32, 8, 128), F32),
            V((8, 48, 128), F32), V((8, 48, 128), F32), V((48, 128), F32), V((32, 1, 128), F32),
            V((1, 128), F32), V((8, 1, 128), F32),
            pltpu.SemaphoreType.DMA((12,)), pltpu.SemaphoreType.DMA((10,)),
            pltpu.SemaphoreType.DMA((10,)), pltpu.SemaphoreType.DMA((3, 4)), pltpu.SemaphoreType.DMA((3, 4)),
        ],
        compiler_params=pltpu.CompilerParams(
            collective_id=0, has_side_effects=True, vmem_limit_bytes=48 * 1024 * 1024
        ),
        name="iteration",
    )(*(pltpu.with_memory_space_constraint(value, pltpu.HBM) for value in (
        face_lists[0, 0], jnp.transpose(block_pattern, (0, 3, 1, 2))[0], multiplicity[0], primal_map[0],
        prev_dot.reshape(1, CASES), residual[0, 0], prev_direction[0, 0], solution[0, 0],
        schur[0, 0], neumann_inverse[0, 0], coarse_basis[0, 0], coarse_inverse,
    )))
    outs = pl.pallas_call(
        deliver,
        out_shape=(field, field, field),
        in_specs=[anywhere] * 3,
        out_specs=(hbm, hbm, hbm),
        scratch_shapes=[pltpu.SemaphoreType.DMA((3,))],
        compiler_params=pltpu.CompilerParams(vmem_limit_bytes=1024 * 1024),
        name="deliver",
    )(*outs)
    return tuple(out[None, None] for out in outs)


def solution(mesh):
    field = P("row", "col", None, None, None)
    return jax.shard_map(
        per_device,
        mesh=mesh,
        in_specs=(
            field, field, field, P(), P("row", "col", None, None), P("row", "col", None), P("row", "col", None, None),
            P("row", "col", None, None, None, None), P("row", "col", None, None, None, None),
            P("row", "col", None, None), P("row", "col", None), P("col", None),
        ),
        out_specs=(field, field, field),
        check_vma=False,
    )
```

time: 63.2 us -> 50.2 us (0.79)
  local copies, waits for them, and re-layouts: 10.5 us -> 0 us
  Pallas kernels: 51.7 us -> 49.5 us
    unnamed x19 -> x0, local copies, waits for them, and re-layouts: 9.75 us -> none
    pallas_call x1 -> x2, Pallas kernels: 51.7 us -> 49.5 us  [the longest x1 47.8 us: per_device(): pl.pallas_call(iteration, out_shape=(pltpu.VMEM((BLOCKS, DOFS, CASES), F3...]
    squeeze x1 -> x0, local copies, waits for them, and re-layouts: 0.76 us -> none  [per_device(): block_pattern[0, 0]]
where the time goes in v2:
time: 50.2 us; the launch traced here: 50.1 us
  Pallas kernels  49.5 us (99%)
  between operations  0.64 us (1%)
    pallas_call x1, Pallas kernels, per_device(): pl.pallas_call(iteration, out_shape=(pltpu.VMEM((BLOCKS, DOFS, CASES), F3...  47.8 us
    pallas_call x1, Pallas kernels, per_device(): pl.pallas_call(deliver, out_shape=(field, field, field), in_specs=[anywhe...  1.69 us

profile of v2, /device:TPU:1, one launch (start us, length us, event | category | flops | bytes accessed | tf_op | source)
XLA Modules:
  0.0 50.1 jit_solution(6795999628955906841)
XLA Ops:
  0.6 47.8 %iteration.1 = (f32[16,128,128]{2,1,0:T(8,128)S(1)}, f32[16,128,128]{2,1,0:T(8,128)S(1)}, f32[16,128,128]{2,1,0:T(8,128)S(1)}) custom-call(s32[4,4]{1,0:T(4,128)} %bitcast.22, s32[3,1,16]{2,1,0:T(1,128)} %bitcast.23, s32[1,16]{1,0:T(1,128)} %bitcast.24, s32[1,8]{1,0:T(1,128)} %bitcast.25, f32[1,128]{1,0:T(1,128)} %bitcast.26, f32[16,128,128]{2,1,0:T(8,128)} %bitcast.18, ...), custom_call_target="tpu_custom_call" | custom-call | tf_op jit(solution)/shard_map/iteration/pallas_call | solution.py:409
  48.4 1.7 %deliver.1 = (f32[16,128,128]{2,1,0:T(8,128)}, f32[16,128,128]{2,1,0:T(8,128)}, f32[16,128,128]{2,1,0:T(8,128)}) custom-call(f32[16,128,128]{2,1,0:T(8,128)S(1)} %get-tuple-element.9.a, f32[16,128,128]{2,1,0:T(8,128)S(1)} %get-tuple-element.10.b, f32[16,128,128]{2,1,0:T(8,128)S(1)} %get-tuple-element.11.c), custom_call_target="tpu_custom_call" | custom-call | tf_op jit(solution)/shard_map/deliver/pallas_call | solution.py:441

commit v3 on v2

--- a/solution.py
+++ b/solution.py
@@ -10,6 +10,7 @@
 BF16 = jnp.bfloat16
 ROWS, COLS = 8, 32
 BLOCKS, DOFS, CASES, SLOTS, PRIMALS = 16, 128, 128, 4, 8
+CHUNKS = 4
 OWNED = 32
 COARSE = OWNED * COLS
 OPPOSITE = (1, 0, 3, 2)
@@ -28,15 +29,21 @@
     return jnp.concatenate(split(values), axis=1)
 
 
+def tile(values):
+    high, low = split(values)
+    top = jnp.concatenate([high, low], axis=1)
+    return jnp.concatenate([top, jnp.concatenate([high, jnp.zeros_like(low)], axis=1)], axis=0)
+
+
 def iteration(
     faces_h, pattern_h, mult_h, pmap_h, prev_dot_h,
     residual_h, previous_h, solution_h, schur_h, neumann_h, basis_h, inverse_h,
-    new_solution, out_res, out_dir,
+    solution, residual, out_image, out_dir, step,
     faces, pattern, mult, pmap, prev_dot,
     nonface, sigma, place, slot_pat,
-    residual, previous, solution, schur, neumann, basis, tiles, inverse,
-    scaled, local, schur_hi, schur_lo, lifted, spread, chosen, picker,
-    direct, direct_hl, image,
+    previous, schur, neumann, basis, tiles, inverse,
+    scaled, local, stiff, lifted, spread, chosen, picker,
+    direct, tiles_hl, image,
     map_got, near_own, near_got,
     face_basis, got_basis, got_local, got_image,
     a_buf, b_own, b_got, c_buf, e_own, e_got, coarse, v_buf, w_own, w_got,
@@ -270,9 +277,8 @@
 
     def order_schur(s, carry):
         b = sigma[s]
-        high, low = split(jnp.concatenate([schur[b, k] for k in range(3)], axis=1))
-        schur_hi[s] = high
-        schur_lo[s] = low
+        for k in range(3):
+            stiff[s, :, 2 * k * DOFS : 2 * (k + 1) * DOFS] = wide(schur[b, k])
         return carry
 
     lax.fori_loop(0, BLOCKS, order_schur, 0)
@@ -329,19 +335,20 @@
             s = face * 4 + k
             value = local[face, k] + mm(lifted[s], right) + mix * previous[sigma[s]]
             direct[s] = value
-            direct_hl[s] = wide(value)
+            tiles_hl[s] = tile(value)
 
     total = jnp.zeros((8, CASES), F32)
     for face in (2, 3, 0, 1):
         def image_row(k, total):
             s = face * 4 + k
-            values = jnp.concatenate([direct_hl[slot_pat[s, n]] for n in range(3)], axis=0)
-            both = mm(schur_hi[s], values)
-            row = both[:, 0:CASES] + both[:, CASES:] + mm(schur_lo[s], values[:, 0:CASES])
+            both = mm(stiff[s, :, 0:256], tiles_hl[slot_pat[s, 0]])
+            both = both + mm(stiff[s, :, 256:512], tiles_hl[slot_pat[s, 1]])
+            both = both + mm(stiff[s, :, 512:768], tiles_hl[slot_pat[s, 2]])
+            row = both[:, 0:CASES] + both[:, CASES:]
             image[face, k] = row
             return total + jnp.sum((direct[s] * row).reshape(16, 8, CASES), axis=0)
 
-        total = lax.fori_loop(0, SLOTS, image_row, total, unroll=2)
+        total = lax.fori_loop(0, SLOTS, image_row, total, unroll=True)
 
     v_buf[j] = jnp.sum(total, axis=0, keepdims=True)
     push(v_buf.at[j], v_buf.at[j], col_ids, 8)
@@ -359,25 +366,19 @@
     w_own[...] = jnp.sum(v_buf[...], axis=0)
     w_got[i] = w_own[...]
     push(w_own, w_got.at[i], row_ids, 9)
-    await_bytes(w_got, ROWS - 1, recv_sem.at[9])
-    step_size = precond_dot / jnp.sum(w_got[...], axis=0)
-
-    def move(b, carry):
-        new_solution[b] = solution[b] + step_size * out_dir[b]
-        return carry
-
-    lax.fori_loop(0, BLOCKS, move, 0)
 
     for face in range(4):
         await_bytes(got_image.at[face], SLOTS, face_recv.at[2, face])
 
-    def finish(b, carry):
+    def order_image(b, carry):
         s = place[b]
-        full = image[s // 4, lax.rem(s, 4)] + used(s) * got_image[s // 4, lax.rem(s, 4)]
-        out_res[b] = residual[b] - step_size * full
-        return carry
-
-    lax.fori_loop(0, BLOCKS, finish, 0)
+        out_image[b] = image[s // 4, lax.rem(s, 4)] + used(s) * got_image[s // 4, lax.rem(s, 4)]
+        return carry
+
+    lax.fori_loop(0, BLOCKS, order_image, 0)
+
+    await_bytes(w_got, ROWS - 1, recv_sem.at[9])
+    step[...] = precond_dot / jnp.sum(w_got[...], axis=0)
 
     for buffer, count, stage in (
         (map_got, 7, 0), (a_buf, 7, 1), (map_got, 24, 2), (a_buf, 24, 3), (near_got, 7, 4), (b_got, 7, 5),
@@ -389,10 +390,21 @@
         await_bytes(image.at[face], SLOTS, face_send.at[2, face])
 
 
-def deliver(a, b, c, a_out, b_out, c_out, sem):
-    copies = [pltpu.make_async_copy(s, t, sem.at[n]) for n, (s, t) in enumerate(((a, a_out), (b, b_out), (c, c_out)))]
-    for copy in copies:
-        copy.start()
+def deliver(
+    solution, residual, image, direction, step, new_solution, new_residual, new_direction,
+    moved, left, sem,
+):
+    copies = [pltpu.make_async_copy(direction, new_direction, sem.at[0, 0])]
+    copies[0].start()
+    step_rows = jnp.broadcast_to(step[...], (DOFS, CASES))
+    for part in range(CHUNKS):
+        blocks = pl.ds(part * (BLOCKS // CHUNKS), BLOCKS // CHUNKS)
+        for b in range(part * (BLOCKS // CHUNKS), (part + 1) * (BLOCKS // CHUNKS)):
+            moved[b] = solution[b] + step_rows * direction[b]
+            left[b] = residual[b] - step_rows * image[b]
+        for n, (source, target) in enumerate(((moved, new_solution), (left, new_residual))):
+            copies.append(pltpu.make_async_copy(source.at[blocks], target.at[blocks], sem.at[n + 1, part]))
+            copies[-1].start()
     for copy in copies:
         copy.wait()
 
@@ -403,24 +415,24 @@
 ):
     field = jax.ShapeDtypeStruct((BLOCKS, DOFS, CASES), F32)
     hbm = pl.BlockSpec(memory_space=pltpu.HBM)
-    anywhere = pl.BlockSpec(memory_space=pl.ANY)
+    vmem = pl.BlockSpec(memory_space=pltpu.VMEM)
     V = pltpu.VMEM
     tall = (4, SLOTS, DOFS, CASES)
     outs = pl.pallas_call(
         iteration,
-        out_shape=(pltpu.VMEM((BLOCKS, DOFS, CASES), F32),) * 3,
+        out_shape=(pltpu.VMEM((BLOCKS, DOFS, CASES), F32),) * 4 + (pltpu.VMEM((1, CASES), F32),),
         in_specs=[hbm] * 12,
-        out_specs=(pl.BlockSpec(memory_space=pltpu.VMEM),) * 3,
+        out_specs=(vmem,) * 5,
         scratch_shapes=[
             pltpu.SMEM((4, 4), jnp.int32), pltpu.SMEM((3, 1, 16), jnp.int32), pltpu.SMEM((1, 16), jnp.int32),
             pltpu.SMEM((1, 8), jnp.int32), V((1, 128), F32),
             pltpu.SMEM((16,), jnp.int32), pltpu.SMEM((16,), jnp.int32), pltpu.SMEM((16,), jnp.int32),
             pltpu.SMEM((16, 3), jnp.int32),
-            V((16, 128, 128), F32), V((16, 128, 128), F32), V((16, 128, 128), F32),
+            V((16, 128, 128), F32),
             V((16, 3, 128, 128), F32), V((16, 3, 128, 128), F32), V((8, 2048), F32), V((16, 8, 128), F32), V((32, 1024), F32),
-            V((16, 128, 256), BF16), V(tall, F32), V((16, 128, 384), BF16), V((16, 128, 384), BF16),
+            V((16, 128, 256), BF16), V(tall, F32), V((16, 128, 768), BF16),
             V((16, 128, 128), BF16), V((8, 32, 128), F32), V((128, 256), BF16), V((256, 256), BF16),
-            V((16, 128, 128), F32), V((16, 128, 256), BF16), V(tall, F32),
+            V((16, 128, 128), F32), V((16, 256, 256), BF16), V(tall, F32),
             V((32, 1, 128), F32), V((1, 128), F32), V((8, 1, 128), F32),
             V((4, 4, 8, 128), F32), V((4, 4, 8, 128), F32), V(tall, F32), V(tall, F32),
             V((32, 8, 128), F32), V((8, 8, 128), F32), V((8, 8, 128), F32), V((32, 8, 128), F32),
@@ -441,10 +453,13 @@
     outs = pl.pallas_call(
         deliver,
         out_shape=(field, field, field),
-        in_specs=[anywhere] * 3,
+        in_specs=[vmem] * 5,
         out_specs=(hbm, hbm, hbm),
-        scratch_shapes=[pltpu.SemaphoreType.DMA((3,))],
-        compiler_params=pltpu.CompilerParams(vmem_limit_bytes=1024 * 1024),
+        scratch_shapes=[
+            pltpu.VMEM((BLOCKS, DOFS, CASES), F32), pltpu.VMEM((BLOCKS, DOFS, CASES), F32),
+            pltpu.SemaphoreType.DMA((3, CHUNKS)),
+        ],
+        compiler_params=pltpu.CompilerParams(vmem_limit_bytes=4 * 1024 * 1024),
         name="deliver",
     )(*outs)
     return tuple(out[None, None] for out in outs)

time: 50.2 us -> 48.4 us (0.964)
  Pallas kernels: 49.5 us -> 47.7 us
    pallas_call x1, Pallas kernels: 47.8 us -> 45.9 us  [per_device(): pl.pallas_call(iteration, out_shape=(pltpu.VMEM((BLOCKS, DOFS, CASES), F3...]
where the time goes in v3:
time: 48.4 us; the launch traced here: 48.3 us
  Pallas kernels  47.7 us (99%)
  between operations  0.64 us (1%)
    pallas_call x1, Pallas kernels, per_device(): pl.pallas_call(iteration, out_shape=(pltpu.VMEM((BLOCKS, DOFS, CASES), F3...  45.9 us
    pallas_call x1, Pallas kernels, per_device(): pl.pallas_call(deliver, out_shape=(field, field, field), in_specs=[vmem]...  1.76 us

profile of v3, /device:TPU:1, one launch (start us, length us, event | category | flops | bytes accessed | tf_op | source)
XLA Modules:
  0.0 48.3 jit_solution(8352808051315247552)
XLA Ops:
  0.6 45.9 %iteration.1 = (f32[16,128,128]{2,1,0:T(8,128)S(1)}, f32[16,128,128]{2,1,0:T(8,128)S(1)}, f32[16,128,128]{2,1,0:T(8,128)S(1)}, f32[16,128,128]{2,1,0:T(8,128)S(1)}, f32[1,128]{1,0:T(1,128)S(1)}) custom-call(s32[4,4]{1,0:T(4,128)} %bitcast.22, s32[3,1,16]{2,1,0:T(1,128)} %bitcast.23, s32[1,16]{1,0:T(1,128)} %bitcast.24, s32[1,8]{1,0:T(1,128)} %bitcast.25, ...), custom_call_target="tpu_custom_call" | custom-call | tf_op jit(solution)/shard_map/iteration/pallas_call | solution.py:421
  46.5 1.8 %deliver.1 = (f32[16,128,128]{2,1,0:T(8,128)}, f32[16,128,128]{2,1,0:T(8,128)}, f32[16,128,128]{2,1,0:T(8,128)}) custom-call(f32[16,128,128]{2,1,0:T(8,128)S(1)} %get-tuple-element.11.solution, f32[16,128,128]{2,1,0:T(8,128)S(1)} %get-tuple-element.12.residual, f32[16,128,128]{2,1,0:T(8,128)S(1)} %get-tuple-element.13.image, ...), custom_call_target="tpu_custom_call" | custom-call | tf_op jit(solution)/shard_map/deliver/pallas_call | solution.py:453

commit v4 on v3

--- a/solution.py
+++ b/solution.py
@@ -42,12 +42,12 @@
     faces, pattern, mult, pmap, prev_dot,
     nonface, sigma, place, slot_pat,
     previous, schur, neumann, basis, tiles, inverse,
-    scaled, local, stiff, lifted, spread, chosen, picker,
+    scaled, local, stiff, lifted, chosen, picker,
     direct, tiles_hl, image,
     map_got, near_own, near_got,
     face_basis, got_basis, got_local, got_image,
     a_buf, b_own, b_got, c_buf, e_own, e_got, coarse, v_buf, w_own, w_got,
-    load_sem, send_sem, recv_sem, face_send, face_recv,
+    load_sem, part_sem, send_sem, recv_sem, face_send, face_recv,
 ):
     i = lax.axis_index("row")
     j = lax.axis_index("col")
@@ -71,7 +71,15 @@
         (schur_h, schur), (previous_h, previous), (solution_h, solution), (prev_dot_h, prev_dot),
     )
     loads = [pltpu.make_async_copy(source, target, load_sem.at[n]) for n, (source, target) in enumerate(pairs)]
-    for n in range(6):
+    parts = [
+        pltpu.make_async_copy(residual_h.at[pl.ds(4 * n, 4)], residual.at[pl.ds(4 * n, 4)], part_sem.at[n]) for n in range(4)
+    ]
+    loads[5].start()
+    parts[0].start()
+    loads[2].start()
+    for n in range(1, 4):
+        parts[n].start()
+    for n in (3, 0, 1):
         loads[n].start()
 
     barrier = pltpu.get_barrier_semaphore()
@@ -106,29 +114,30 @@
             device_id=face_id[face], device_id_type=MESH,
         ).start()
 
-    for n in (2, 3):
-        loads[n].wait()
+    loads[2].wait()
     weight = lambda b: jnp.where(mult[0, b] == 2, F32(0.5), F32(1.0))
     used = lambda s: jnp.where(faces[s // 4, s % 4] < BLOCKS, F32(1.0), F32(0.0))
 
     lanes = lax.broadcasted_iota(jnp.int32, (1, 128), 1)
-    own_map = jnp.zeros((1, 128), jnp.int32)
-    for p in range(PRIMALS):
-        own_map = jnp.where(lax.rem(lanes, 8) == p, pmap[0, p], own_map)
     home = x * 8 + z
-    map_got[home] = own_map.astype(F32)
-
-    loads[4].wait()
+
     loads[5].wait()
 
     both = jnp.zeros((16, 2 * CASES), F32)
     for b in range(0, BLOCKS, 2):
+        if b % 4 == 0:
+            parts[b // 4].wait()
         for n in (b, b + 1):
             scaled[n] = wide(residual[n] * weight(n))
         left = jnp.concatenate(split(basis[:, b * DOFS : (b + 2) * DOFS]), axis=0)
         both = both + mm(left, scaled[pl.ds(b, 2)].reshape(2 * DOFS, 2 * CASES))
     a_buf[home] = both[0:8, 0:CASES] + both[0:8, CASES:] + both[8:16, 0:CASES]
 
+    loads[3].wait()
+    own_map = jnp.zeros((1, 128), jnp.int32)
+    for p in range(PRIMALS):
+        own_map = jnp.where(lax.rem(lanes, 8) == p, pmap[0, p], own_map)
+    map_got[home] = own_map.astype(F32)
     pl.semaphore_wait(barrier, 17)
     push(map_got.at[home], map_got.at[home], z_ids, 0)
     push(a_buf.at[home], a_buf.at[home], z_ids, 1)
@@ -137,6 +146,14 @@
 
     for n in (0, 1):
         loads[n].wait()
+
+    def send_part(face, first, count):
+        part = pl.ds(first, count)
+        pltpu.make_async_remote_copy(
+            src_ref=image.at[face, part], dst_ref=got_image.at[OPPOSITE[face], part],
+            send_sem=face_send.at[2, face], recv_sem=face_recv.at[2, OPPOSITE[face]],
+            device_id=face_id[face], device_id_type=MESH,
+        ).start()
 
     def find_nonface(b, count):
         on_face = faces[0, 0] == b
@@ -257,18 +274,19 @@
             line = jnp.where(lanes // 32 == t, near_got[half * 4 + t], line)
         line = line.astype(jnp.int32)
         here = jnp.logical_and(line >= 0, lax.rem(line // 4, 8) == i)
-        where_at = jnp.where(here, (line // OWNED) * 8 + lax.rem(line, 4), -1)
+        where_at = jnp.where(here, lax.rem(line, 4) * COLS + line // OWNED, -1)
         for quarter_rows in range(2):
             rows = lax.broadcasted_iota(jnp.int32, (128, 128), 0) + quarter_rows * 128
-            hit = jnp.logical_or(rows == where_at, jnp.logical_and(line == -1, lax.rem(rows, 8) == 4))
+            hit = jnp.logical_or(rows == where_at, jnp.logical_and(line == -1, rows // COLS == 4))
             hot = jnp.where(hit, F32(1.0), F32(0.0))
             picker[pl.ds(half * 128, 128), pl.ds(quarter_rows * 128, 128)] = jnp.transpose(hot).astype(BF16)
 
     await_bytes(b_got, ROWS - 1, recv_sem.at[5])
     held = jnp.sum(b_got[...], axis=0)
     dot = 0.5 * jnp.sum(held * pltpu.roll(held, 4, 0), axis=0, keepdims=True) + local_dot
-    rows = lax.broadcasted_iota(jnp.int32, (8, CASES), 0)
-    c_buf[j] = jnp.where(rows < 4, held, jnp.where(rows == 4, jnp.broadcast_to(dot, (8, CASES)), F32(0.0)))
+    for q in range(4):
+        c_buf[j, :, q * CASES : (q + 1) * CASES] = held[q : q + 1]
+    c_buf[j, :, 4 * CASES :] = dot
     push(c_buf.at[j], c_buf.at[j], col_ids, 6)
     for face in (2, 3, 0, 1):
         send_face(local.at[face], got_local, face, 1)
@@ -300,13 +318,15 @@
     lax.fori_loop(0, BLOCKS, lift, 0)
 
     await_bytes(c_buf, COLS - 1, recv_sem.at[6])
-    both = mm(picker[...], wide(c_buf[...].reshape(COLS * 8, CASES)))
-    spread[...] = (both[:, 0:CASES] + both[:, CASES:]).reshape(ROWS, 32, CASES)
+    rows_held = [c_buf[:, :, q * CASES : (q + 1) * CASES].reshape(COLS, CASES) for q in range(5)]
+    both = mm(picker[...], wide(jnp.concatenate(rows_held + [jnp.zeros((96, CASES), F32)], axis=0)))
+    rows_for = both[:, 0:CASES] + both[:, CASES:]
     for t in range(ROWS):
-        e_own[t, 0:8] = spread[t, 0:8]
-        e_own[t, 8:16] = spread[(t + 7) % ROWS, 0:8]
-        e_own[t, 16:24] = spread[(t + 1) % ROWS, 0:8]
-        e_own[t, 24:48] = spread[t, 8:32]
+        north, south = (t + 7) % ROWS * 32, (t + 1) % ROWS * 32
+        e_own[t, 0:8] = rows_for[t * 32 : t * 32 + 8]
+        e_own[t, 8:16] = rows_for[north : north + 8]
+        e_own[t, 16:24] = rows_for[south : south + 8]
+        e_own[t, 24:48] = rows_for[t * 32 + 8 : t * 32 + 32]
     e_got[i] = e_own[i]
     scatter_row(e_own, e_got, 7)
     for face in range(4):
@@ -352,8 +372,10 @@
 
     v_buf[j] = jnp.sum(total, axis=0, keepdims=True)
     push(v_buf.at[j], v_buf.at[j], col_ids, 8)
-    for face in (2, 3, 0, 1):
-        send_face(image.at[face], got_image, face, 2)
+    for face in (2, 3):
+        send_part(face, 0, 3)
+    for face in (0, 1):
+        send_part(face, 0, 4)
 
     def order_direction(b, carry):
         out_dir[b] = direct[place[b]]
@@ -366,6 +388,8 @@
     w_own[...] = jnp.sum(v_buf[...], axis=0)
     w_got[i] = w_own[...]
     push(w_own, w_got.at[i], row_ids, 9)
+    for face in (2, 3):
+        send_part(face, 3, 1)
 
     for face in range(4):
         await_bytes(got_image.at[face], SLOTS, face_recv.at[2, face])
@@ -377,17 +401,19 @@
 
     lax.fori_loop(0, BLOCKS, order_image, 0)
 
-    await_bytes(w_got, ROWS - 1, recv_sem.at[9])
-    step[...] = precond_dot / jnp.sum(w_got[...], axis=0)
-
     for buffer, count, stage in (
         (map_got, 7, 0), (a_buf, 7, 1), (map_got, 24, 2), (a_buf, 24, 3), (near_got, 7, 4), (b_got, 7, 5),
-        (c_buf, 31, 6), (e_got, 7, 7), (v_buf, 31, 8), (w_got, 7, 9),
+        (c_buf, 31, 6), (e_got, 7, 7), (v_buf, 31, 8),
     ):
         await_bytes(buffer, count, send_sem.at[stage])
     for face in range(4):
         await_bytes(face_basis.at[face], SLOTS, face_send.at[0, face])
         await_bytes(image.at[face], SLOTS, face_send.at[2, face])
+
+    await_bytes(w_got, ROWS - 1, recv_sem.at[9])
+    step[...] = precond_dot / jnp.sum(w_got[...], axis=0)
+
+    await_bytes(w_got, ROWS - 1, send_sem.at[9])
 
 
 def deliver(
@@ -431,14 +457,14 @@
             V((16, 128, 128), F32),
             V((16, 3, 128, 128), F32), V((16, 3, 128, 128), F32), V((8, 2048), F32), V((16, 8, 128), F32), V((32, 1024), F32),
             V((16, 128, 256), BF16), V(tall, F32), V((16, 128, 768), BF16),
-            V((16, 128, 128), BF16), V((8, 32, 128), F32), V((128, 256), BF16), V((256, 256), BF16),
+            V((16, 128, 128), BF16), V((128, 256), BF16), V((256, 256), BF16),
             V((16, 128, 128), F32), V((16, 256, 256), BF16), V(tall, F32),
             V((32, 1, 128), F32), V((1, 128), F32), V((8, 1, 128), F32),
             V((4, 4, 8, 128), F32), V((4, 4, 8, 128), F32), V(tall, F32), V(tall, F32),
-            V((32, 8, 128), F32), V((8, 8, 128), F32), V((8, 8, 128), F32), V((32, 8, 128), F32),
+            V((32, 8, 128), F32), V((8, 8, 128), F32), V((8, 8, 128), F32), V((32, 1, 640), F32),
             V((8, 48, 128), F32), V((8, 48, 128), F32), V((48, 128), F32), V((32, 1, 128), F32),
             V((1, 128), F32), V((8, 1, 128), F32),
-            pltpu.SemaphoreType.DMA((12,)), pltpu.SemaphoreType.DMA((10,)),
+            pltpu.SemaphoreType.DMA((12,)), pltpu.SemaphoreType.DMA((4,)), pltpu.SemaphoreType.DMA((10,)),
             pltpu.SemaphoreType.DMA((10,)), pltpu.SemaphoreType.DMA((3, 4)), pltpu.SemaphoreType.DMA((3, 4)),
         ],
         compiler_params=pltpu.CompilerParams(

time: 48.4 us -> 47.2 us (0.975)
  Pallas kernels: 47.7 us -> 46.4 us
    pallas_call x1, Pallas kernels: 45.9 us -> 44.6 us  [per_device(): pl.pallas_call(iteration, out_shape=(pltpu.VMEM((BLOCKS, DOFS, CASES), F3...]
where the time goes in v4:
time: 47.2 us; the launch traced here: 47 us
  Pallas kernels  46.4 us (98%)
  between operations  0.64 us (1%)
    pallas_call x1, Pallas kernels, per_device(): pl.pallas_call(iteration, out_shape=(pltpu.VMEM((BLOCKS, DOFS, CASES), F3...  44.6 us
    pallas_call x1, Pallas kernels, per_device(): pl.pallas_call(deliver, out_shape=(field, field, field), in_specs=[vmem]...  1.76 us

profile of v4, /device:TPU:1, one launch (start us, length us, event | category | flops | bytes accessed | tf_op | source)
XLA Modules:
  0.0 47.0 jit_solution(17721483280008650187)
XLA Ops:
  0.6 44.6 %iteration.1 = (f32[16,128,128]{2,1,0:T(8,128)S(1)}, f32[16,128,128]{2,1,0:T(8,128)S(1)}, f32[16,128,128]{2,1,0:T(8,128)S(1)}, f32[16,128,128]{2,1,0:T(8,128)S(1)}, f32[1,128]{1,0:T(1,128)S(1)}) custom-call(s32[4,4]{1,0:T(4,128)} %bitcast.22, s32[3,1,16]{2,1,0:T(1,128)} %bitcast.23, s32[1,16]{1,0:T(1,128)} %bitcast.24, s32[1,8]{1,0:T(1,128)} %bitcast.25, ...), custom_call_target="tpu_custom_call" | custom-call | tf_op jit(solution)/shard_map/iteration/pallas_call | solution.py:447
  45.3 1.8 %deliver.1 = (f32[16,128,128]{2,1,0:T(8,128)}, f32[16,128,128]{2,1,0:T(8,128)}, f32[16,128,128]{2,1,0:T(8,128)}) custom-call(f32[16,128,128]{2,1,0:T(8,128)S(1)} %get-tuple-element.11.solution, f32[16,128,128]{2,1,0:T(8,128)S(1)} %get-tuple-element.12.residual, f32[16,128,128]{2,1,0:T(8,128)S(1)} %get-tuple-element.13.image, ...), custom_call_target="tpu_custom_call" | custom-call | tf_op jit(solution)/shard_map/deliver/pallas_call | solution.py:479

commit v5 on v4

--- a/solution.py
+++ b/solution.py
@@ -61,7 +61,7 @@
     z_ids = [(i, z_at[t] + x) for t in z_far]
     x_ids = [(i, z * 4 + x_at[t]) for t in x_far]
     hops = lambda t: min(t[0], 8 - t[0]) + min(t[1], 4 - t[1])
-    offsets = sorted(((dz, dx) for dz in range(8) for dx in range(4) if dz or dx), key=lambda t: -hops(t))
+    offsets = sorted(((dz, dx) for dz in range(8) for dx in range(4) if dz or dx), key=lambda t: (-min(t[0], 8 - t[0]), -min(t[1], 4 - t[1])))
     col_ids = [(i, z_at[dz] + x_at[dx]) for dz, dx in offsets]
     row_ids = [row_id(t) for t in (4, 5, 3, 6, 2, 7, 1)]
 

time: 47.2 us -> 47.2 us (level)
  no operation moved by 1% of the time
where the time goes in v5:
time: 47.2 us; the launch traced here: 47 us
  Pallas kernels  46.4 us (98%)
  between operations  0.64 us (1%)
    pallas_call x1, Pallas kernels, per_device(): pl.pallas_call(iteration, out_shape=(pltpu.VMEM((BLOCKS, DOFS, CASES), F3...  44.6 us
    pallas_call x1, Pallas kernels, per_device(): pl.pallas_call(deliver, out_shape=(field, field, field), in_specs=[vmem]...  1.76 us

profile of v5, /device:TPU:1, one launch (start us, length us, event | category | flops | bytes accessed | tf_op | source)
XLA Modules:
  0.0 47.0 jit_solution(3292635150147011793)
XLA Ops:
  0.6 44.6 %iteration.1 = (f32[16,128,128]{2,1,0:T(8,128)S(1)}, f32[16,128,128]{2,1,0:T(8,128)S(1)}, f32[16,128,128]{2,1,0:T(8,128)S(1)}, f32[16,128,128]{2,1,0:T(8,128)S(1)}, f32[1,128]{1,0:T(1,128)S(1)}) custom-call(s32[4,4]{1,0:T(4,128)} %bitcast.22, s32[3,1,16]{2,1,0:T(1,128)} %bitcast.23, s32[1,16]{1,0:T(1,128)} %bitcast.24, s32[1,8]{1,0:T(1,128)} %bitcast.25, ...), custom_call_target="tpu_custom_call" | custom-call | tf_op jit(solution)/shard_map/iteration/pallas_call | solution.py:447
  45.2 1.8 %deliver.1 = (f32[16,128,128]{2,1,0:T(8,128)}, f32[16,128,128]{2,1,0:T(8,128)}, f32[16,128,128]{2,1,0:T(8,128)}) custom-call(f32[16,128,128]{2,1,0:T(8,128)S(1)} %get-tuple-element.11.solution, f32[16,128,128]{2,1,0:T(8,128)S(1)} %get-tuple-element.12.residual, f32[16,128,128]{2,1,0:T(8,128)S(1)} %get-tuple-element.13.image, ...), custom_call_target="tpu_custom_call" | custom-call | tf_op jit(solution)/shard_map/deliver/pallas_call | solution.py:479
